TPU v7x, 32 devices: a whole 2x2x4 slice. The times are simulated.
32 devices in a mesh: leaf: 8 (over z, x), rhs: 4 (over y, core).
Axes of the slice: x: 2, y: 2, z: 4, core: 2. Of those that a mesh axis runs over, the one named last changes fastest.
Arguments:
- coords: bfloat16 [64, 32768], P(None, 'leaf'), may hold values from -1.5 to 1.5
- rhs: bfloat16 [256, 32768], P('rhs', 'leaf'), parts along dimension 0, may hold values from -6 to 6
- basis: bfloat16 [64, 512, 256], P('leaf'), may hold values from -0.25 to 0.25
- transfer_one: bfloat16 [32, 512, 256], P('leaf'), may hold values from -0.25 to 0.25
- transfer_two: bfloat16 [16, 512, 256], P('leaf'), may hold values from -0.25 to 0.25
- far_blocks: bfloat16 [112, 4, 256, 256], P('leaf'), may hold values from -0.375 to 0.375
- neighbours: int32 [64, 8], replicated, may hold values from 0 to 63, as said below
- far_lists: int32 [112, 4], replicated, may hold values from 0 to 111, as said below
Outputs:
- product: float32 [256, 32768], P('rhs', 'leaf'), parts along dimension 0
There are 4 independent parts, one for each index of `rhs`. A program takes and returns all parts, laid end to end along the dimension named above; an argument that names none is the same for every part. Nothing has to cross between parts.
Inputs may be any that keep to these rules, and one draw needn't show every extreme that they name: `neighbours`: row i starts with leaf i itself; its other entries name leaves of other devices (leaf i lies on device i // 8). The entries after the first in the lists of one device's leaves name no other device more than 8 times, and the leaves of every device are named exactly 56 times by such entries over all lists. `far_lists`: entry (n, f) names a node of the same level as node n on another device (node n lies on device n // 14). The entries of one device's nodes name no other device more than 8 times, and the nodes of every device are named exactly 56 times over all entries.
All inputs are finite; a program needn't handle non-finite values.
Results may differ from a plain program's by a relative error of at most 0.005.
Values may be sent and summed in bfloat16 or wider, within the bound.
A program may use at most 128 MiB of HBM per device.

v0:
```python
import jax
import jax.numpy as jnp
from jax import lax
from jax.sharding import PartitionSpec as P

FEAT = 64
RANK = 256
R = 64
LEAF = 512
NB = 8
FAR = 4


def kernel_tiles(sources, targets):
    inner = jnp.einsum("...fa,...fb->...ab", sources, targets, preferred_element_type=jnp.float32)
    src_f = sources.astype(jnp.float32)
    dst_f = targets.astype(jnp.float32)
    src_sq = jnp.sum(src_f * src_f, axis=-2)
    dst_sq = jnp.sum(dst_f * dst_f, axis=-2)
    return jnp.exp(inner - 0.5 * src_sq[..., :, None] - 0.5 * dst_sq[..., None, :]).astype(
        jnp.bfloat16
    )


def tile_products(sources, targets):
    kernel = kernel_tiles(sources[:, :FEAT], targets)
    return jnp.einsum("gra,gab->grb", sources[:, FEAT:], kernel, preferred_element_type=jnp.float32)


def grouped_products(sources, targets):
    groups = sources.shape[0] // 4
    paired = (
        sources.reshape(groups, 4, sources.shape[1], sources.shape[2]),
        targets.reshape(groups, 4, targets.shape[1], targets.shape[2]),
    )
    outcome = lax.map(lambda couple: tile_products(couple[0], couple[1]), paired)
    return outcome.reshape(sources.shape[0], R, sources.shape[2])


def slot_ranks(owners):
    entry_count = owners.shape[1]
    position = jnp.arange(entry_count, dtype=jnp.int32)
    earlier = position[None, :] < position[:, None]
    matches = owners[:, :, None] == owners[:, None, :]
    return jnp.sum(jnp.logical_and(matches, earlier[None]), axis=2)


def arrivals(owners, ranks, entries, device_index, slot_count):
    entry_count = owners.shape[1]
    located = jnp.nonzero((owners == device_index).reshape(-1), size=entry_count, fill_value=0)[
        0
    ].astype(jnp.int32)
    requester = located // entry_count
    target_slot = requester * slot_count + ranks.reshape(-1)[located]
    return (target_slot, entries.reshape(-1)[located])


def join_pairs(skeleton):
    return skeleton.reshape(-1, 2, R, RANK).transpose(0, 2, 1, 3).reshape(-1, R, 2 * RANK)


def descend(parent, transfer, child_far):
    rounded = parent.astype(jnp.bfloat16)
    spread = jnp.einsum("mrk,mjk->mrj", rounded, transfer, preferred_element_type=jnp.float32)
    spread = spread.reshape(-1, R, 2, RANK).transpose(0, 2, 1, 3).reshape(-1, R, RANK)
    return child_far + spread


def on_device(coords, rhs, basis, transfer_one, transfer_two, far_blocks, neighbours, far_lists):
    peer_count = lax.axis_size("leaf")
    device_index = lax.axis_index("leaf")
    local_leaves = basis.shape[0]
    node_count = far_blocks.shape[0]
    remote_count = (NB - 1) * local_leaves
    near_slots = (remote_count + peer_count - 2) // (peer_count - 1)
    far_count = node_count * FAR
    far_slots = (far_count + peer_count - 2) // (peer_count - 1)
    points = coords.reshape(FEAT, local_leaves, LEAF).transpose(1, 0, 2)
    charges = rhs.reshape(R, local_leaves, LEAF).transpose(1, 0, 2)
    blocks = jnp.concatenate([points, charges], axis=1)
    remote = neighbours.reshape(peer_count, local_leaves, NB)[:, :, 1:].reshape(
        peer_count, remote_count
    )
    owners = remote // local_leaves
    ranks = slot_ranks(owners)
    my_owners = lax.dynamic_index_in_dim(owners, device_index, 0, keepdims=False)
    my_ranks = lax.dynamic_index_in_dim(ranks, device_index, 0, keepdims=False)
    my_slots = my_owners * near_slots + my_ranks
    outgoing, wanted = arrivals(owners, ranks, remote, device_index, near_slots)
    item_leaf = jnp.arange(remote_count, dtype=jnp.int32) // (NB - 1)
    skel_zero = jnp.einsum(
        "lra,lak->lrk", charges, basis, preferred_element_type=jnp.float32
    ).astype(jnp.bfloat16)
    skel_one = jnp.einsum(
        "mrj,mjk->mrk", join_pairs(skel_zero), transfer_one, preferred_element_type=jnp.float32
    ).astype(jnp.bfloat16)
    skel_two = jnp.einsum(
        "mrj,mjk->mrk", join_pairs(skel_one), transfer_two, preferred_element_type=jnp.float32
    ).astype(jnp.bfloat16)
    skeleton = jnp.concatenate([skel_zero, skel_one, skel_two], axis=0)
    far_remote = far_lists.reshape(peer_count, far_count)
    far_owners = far_remote // node_count
    far_ranks = slot_ranks(far_owners)
    far_outgoing, far_wanted = arrivals(far_owners, far_ranks, far_remote, device_index, far_slots)
    far_buffer = (
        jnp.zeros((peer_count * far_slots, R, RANK), jnp.bfloat16)
        .at[far_outgoing]
        .set(skeleton[far_wanted % node_count])
    )
    far_arrived = lax.all_to_all(
        far_buffer.reshape(peer_count, far_slots, R, RANK),
        "leaf",
        split_axis=0,
        concat_axis=0,
        tiled=True,
    )
    my_far = lax.dynamic_index_in_dim(
        far_owners, device_index, 0, keepdims=False
    ) * far_slots + lax.dynamic_index_in_dim(far_ranks, device_index, 0, keepdims=False)
    partners = far_arrived.reshape(peer_count * far_slots, R, RANK)[my_far].reshape(
        node_count, FAR, R, RANK
    )
    leaf_buffer = (
        jnp.zeros((peer_count * near_slots, FEAT + R, LEAF), jnp.bfloat16)
        .at[outgoing]
        .set(blocks[wanted % local_leaves])
    )
    leaf_arrived = lax.all_to_all(
        leaf_buffer.reshape(peer_count, near_slots, FEAT + R, LEAF),
        "leaf",
        split_axis=0,
        concat_axis=0,
        tiled=True,
    )
    sources = leaf_arrived.reshape(peer_count * near_slots, FEAT + R, LEAF)[my_slots]
    per_item = grouped_products(sources, points[item_leaf])
    self_terms = tile_products(blocks, points)
    near = self_terms + jnp.sum(per_item.reshape(local_leaves, NB - 1, R, LEAF), axis=1)
    far = jnp.einsum("nfrk,nfkj->nrj", partners, far_blocks, preferred_element_type=jnp.float32)
    far_zero = far[:local_leaves]
    far_one = far[local_leaves : local_leaves * 3 // 2]
    far_two = far[local_leaves * 3 // 2 :]
    middle = descend(far_two, transfer_two, far_one)
    lowest = descend(middle, transfer_one, far_zero)
    result = near + jnp.einsum(
        "lrk,lak->lra", lowest.astype(jnp.bfloat16), basis, preferred_element_type=jnp.float32
    )
    return result.transpose(1, 0, 2).reshape(R, local_leaves * LEAF)


def solution(mesh):
    return jax.shard_map(
        on_device,
        mesh=mesh,
        in_specs=(
            P(None, "leaf"),
            P("rhs", "leaf"),
            P("leaf", None, None),
            P("leaf", None, None),
            P("leaf", None, None),
            P("leaf", None, None, None),
            P(),
            P(),
        ),
        out_specs=P("rhs", "leaf"),
        check_vma=False,
    )
```

profile of v0, /device:TPU:0, one launch (start us, length us, event | category | flops | bytes accessed | tf_op | source)
XLA Modules:
  0.0 368.2 jit_solution(6124035899294946189)
XLA Ops:
  1.7 1.3 convert_reduce_fusion.3
  4.8 4.0 %scatter_custom_fusion.2 = s32[56]{0:T(128)S(1)} fusion(s32[448]{0:T(512)S(1)} %compare_select_fusion.9, s32[448]{0:T(512)S(1)} %ne.270, s32[]{:T(128)} %copy.107), kind=kCustom, calls=%fused_computation.170 | custom fusion | flops 448 | bytes 228 | tf_op jit(solution)/shard_map/scatter-add | solution.py:50
  13.5 1.5 convolution_convert_fusion
  15.7 2.0 gather_fusion.7
  17.7 1.6 broadcast_in_dim.28
  19.3 9.8 %scatter_fusion.1 = bf16[64,64,256]{2,1,0:T(8,128)(2,1)} fusion(bf16[64,64,256]{2,1,0:T(8,128)(2,1)} %broadcast_in_dim.28, s32[56]{0:T(128)S(1)} %fusion.45, bf16[56,64,256]{2,1,0:T(8,128)(2,1)} %gather_fusion.7), kind=kCustom, calls=%fused_computation.12 | custom fusion | bytes 5505248 | tf_op jit(solution)/shard_map/scatter | solution.py:108
  29.1 7.3 %all-to-all-start.1 = ((bf16[8,8,64,256]{3,2,1,0:T(8,128)(2,1)}), bf16[8,8,64,256]{3,2,1,0:T(8,128)(2,1)}, u32[]{:S(2)}, u32[]{:S(2)}) async-start(bf16[8,8,64,256]{3,2,1,0:T(8,128)(2,1)} %bitcast.110), calls=%async_computation.1 | async-start | bytes 4194304 | tf_op jit(solution)/shard_map/all_to_all | solution.py:110
  37.0 4.0 %scatter_custom_fusion = s32[56]{0:T(128)S(1)} fusion(s32[448]{0:T(512)S(1)} %compare_select_fusion.10, s32[448]{0:T(512)S(1)} %ne.270, s32[]{:T(128)} %copy.107), kind=kCustom, calls=%fused_computation.172 | custom fusion | flops 448 | bytes 228 | tf_op jit(solution)/shard_map/scatter-add | solution.py:50
  44.8 5.2 %gather_fusion.2 = bf16[56,128,512]{2,1,0:T(8,128)(2,1)} fusion(bf16[8,128,512]{2,1,0:T(8,128)(2,1)S(1)} %pad_maximum_fusion, s32[1024]{0:T(1024)S(1)} %pad_clamp_fusion.5), kind=kCustom, calls=%fused_computation.2 | custom fusion | bytes 14680288 | tf_op jit(solution)/shard_map/gather | solution.py:126
  50.8 4.2 %broadcast_in_dim.25 = bf16[64,128,512]{2,1,0:T(8,128)(2,1)} broadcast(bf16[]{:T(256)} %constant.135.clone.1), dimensions={} | broadcast | bytes 8388610 | tf_op jit(solution)/shard_map/broadcast_in_dim | solution.py:124
  55.0 19.5 %scatter_fusion = bf16[64,128,512]{2,1,0:T(8,128)(2,1)} fusion(bf16[64,128,512]{2,1,0:T(8,128)(2,1)} %broadcast_in_dim.25, s32[56]{0:T(128)S(1)} %fusion.41, bf16[56,128,512]{2,1,0:T(8,128)(2,1)} %gather_fusion.2), kind=kCustom, calls=%fused_computation.10 | custom fusion | bytes 22020320 | tf_op jit(solution)/shard_map/scatter | solution.py:126
  74.5 10.2 %all-to-all-done.1 = bf16[8,8,64,256]{3,2,1,0:T(8,128)(2,1)} async-done(((bf16[8,8,64,256]{3,2,1,0:T(8,128)(2,1)}), bf16[8,8,64,256]{3,2,1,0:T(8,128)(2,1)}, u32[]{:S(2)}, u32[]{:S(2)}) %all-to-all-start.1) | async-done | bytes 2097184 | tf_op jit(solution)/shard_map/all_to_all | solution.py:110
  84.7 5.3 %all-to-all-start = ((bf16[8,8,128,512]{3,2,1,0:T(8,128)(2,1)}), bf16[8,8,128,512]{3,2,1,0:T(8,128)(2,1)}, u32[]{:S(2)}, u32[]{:S(2)}) async-start(bf16[8,8,128,512]{3,2,1,0:T(8,128)(2,1)} %bitcast.109), calls=%async_computation | async-start | bytes 16777216 | tf_op jit(solution)/shard_map/all_to_all | solution.py:128
  90.3 2.7 gather_fusion.4
  94.1 3.5 gather_fusion.8
  97.6 5.1 %convolution_bitcast_fusion.1 = f32[14,64,256]{2,1,0:T(8,128)S(1)} fusion(bf16[14,4,64,256]{3,2,1,0:T(8,128)(2,1)} %bitcast.112, bf16[14,4,256,256]{3,2,1,0:T(8,128)(2,1)} %param.15), kind=kOutput, calls=%fused_computation.36 | convolution fusion | flops 469762048 | bytes 10092544 | tf_op jit(solution)/shard_map/nfrk,nfkj->nrj/dot_general | solution.py:139
  104.5 167.6 %all-to-all-done = bf16[8,8,128,512]{3,2,1,0:T(8,128)(2,1)} async-done(((bf16[8,8,128,512]{3,2,1,0:T(8,128)(2,1)}), bf16[8,8,128,512]{3,2,1,0:T(8,128)(2,1)}, u32[]{:S(2)}, u32[]{:S(2)}) %all-to-all-start) | async-done | bytes 8388640 | tf_op jit(solution)/shard_map/all_to_all | solution.py:128
  272.0 8.7 %gather_fusion.3 = bf16[56,128,512]{2,1,0:T(8,128)(2,1)} fusion(bf16[64,128,512]{2,1,0:T(8,128)(2,1)} %bitcast.13, s32[1024]{0:T(1024)S(1)} %pad_clamp_fusion.4), kind=kCustom, calls=%fused_computation.3 | custom fusion | bytes 14680288 | tf_op jit(solution)/shard_map/gather | solution.py:135
  280.7 74.0 %while.10 = (s32[]{:T(128)}, f32[14,4,64,512]{3,2,1,0:T(8,128)}, bf16[14,4,128,512]{3,2,1,0:T(8,128)(2,1)}, bf16[14,4,64,512]{3,2,1,0:T(8,128)(2,1)}, s32[]{:T(128)}) while((s32[]{:T(128)}, f32[14,4,64,512]{3,2,1,0:T(8,128)}, bf16[14,4,128,512]{3,2,1,0:T(8,128)(2,1)}, bf16[14,4,64,512]{3,2,1,0:T(8,128)(2,1)}, s32[]{:T(128)}) %tuple.34), condition=%wide.region_11.12_spmd, body=%wide.region_8.11_spmd.sunk | while | flops 272367616 | bytes 2950213 | solution.py:36
  280.7 1.1 dynamic-slice_bitcast_fusion.2
  282.9 3.1 fusion.91
  286.0 1.1 dynamic-slice_bitcast_fusion.2
  288.2 3.1 fusion.91
  291.3 1.1 dynamic-slice_bitcast_fusion.2
  293.5 3.1 fusion.91
  296.6 1.1 dynamic-slice_bitcast_fusion.2
  298.8 3.1 fusion.91
  301.9 1.1 dynamic-slice_bitcast_fusion.2
  304.1 3.1 fusion.91
  307.1 1.1 dynamic-slice_bitcast_fusion.2
  309.3 3.1 fusion.91
  312.4 1.1 dynamic-slice_bitcast_fusion.2
  314.6 3.1 fusion.91
  317.7 1.1 dynamic-slice_bitcast_fusion.2
  319.9 3.1 fusion.91
  323.0 1.1 dynamic-slice_bitcast_fusion.2
  325.2 3.1 fusion.91
  328.3 1.1 dynamic-slice_bitcast_fusion.2
  330.5 3.1 fusion.91
  333.6 1.1 dynamic-slice_bitcast_fusion.2
  335.8 3.1 fusion.91
  338.8 1.1 dynamic-slice_bitcast_fusion.2
  341.0 3.1 fusion.91
  346.3 3.1 fusion.91
  351.6 3.1 fusion.91
  354.7 5.1 %reduce_sum.81 = f32[8,64,512]{2,1,0:T(8,128)} reduce(f32[8,7,64,512]{3,2,1,0:T(8,128)} %bitcast.113, f32[]{:T(128)} %constant.132.clone.1), dimensions={1}, to_apply=%region_12.13 | reduce | flops 1572864 | bytes 8388612 | tf_op jit(solution)/shard_map/reduce_sum | solution.py:138
  359.8 5.3 %fusion.20 = f32[64,8,512]{2,0,1:T(8,128)} fusion(f32[8,512]{1,0:T(8,128)S(1)} %copy-done.11, f32[8,64,512]{2,1,0:T(8,128)} %reduce_sum.81, bf16[8,8,8,512]{3,2,1,0:T(8,128)(2,1)} %bitcast.121, bf16[8,8,8,512]{3,2,1,0:T(8,128)(2,1)} %bitcast.117), kind=kOutput, calls=%fused_computation.37 | convolution fusion | flops 543424512 | bytes 3162112 | tf_op jit(solution)/shard_map/gra,gab->grb/dot_general | solution.py:27
  365.1 2.0 fusion.19
  (149 shorter events, 35.7 us)
Async XLA Ops:
  0.0 13.5 %copy-start = (bf16[8,512,256]{2,1,0:T(8,128)(2,1)S(1)}, bf16[8,512,256]{2,1,0:T(8,128)(2,1)}, u32[]{:S(2)}) copy-start(bf16[8,512,256]{2,1,0:T(8,128)(2,1)} %param.12) | copy-start | bytes 6291460
  0.0 15.1 %copy-start.3 = (bf16[4,512,256]{2,1,0:T(8,128)(2,1)S(1)}, bf16[4,512,256]{2,1,0:T(8,128)(2,1)}, u32[]{:S(2)}) copy-start(bf16[4,512,256]{2,1,0:T(8,128)(2,1)} %param.13) | copy-start | bytes 3145732
  13.4 2.0 copy-start.6
  19.3 24.5 %copy-start.8 = (bf16[64,4096]{1,0:T(8,128)(2,1)S(1)}, bf16[64,4096]{1,0:T(8,128)(2,1)}, u32[]{:S(2)}) copy-start(bf16[64,4096]{1,0:T(8,128)(2,1)} %param.10) | copy-start | bytes 1572868
  19.3 24.6 %copy-start.10 = (bf16[64,4096]{1,0:T(8,128)(2,1)S(1)}, bf16[64,4096]{1,0:T(8,128)(2,1)}, u32[]{:S(2)}) copy-start(bf16[64,4096]{1,0:T(8,128)(2,1)} %param.11) | copy-start | bytes 1572868
  29.1 55.6 %all-to-all-start.1 = ((bf16[8,8,64,256]{3,2,1,0:T(8,128)(2,1)}), bf16[8,8,64,256]{3,2,1,0:T(8,128)(2,1)}, u32[]{:S(2)}, u32[]{:S(2)}) async-start(bf16[8,8,64,256]{3,2,1,0:T(8,128)(2,1)} %bitcast.110), calls=%async_computation.1 | async-start | bytes 4194304 | tf_op jit(solution)/shard_map/all_to_all | solution.py:110
  44.0 0.8 copy-start.1
  84.7 5.7 %copy-start.2 = (bf16[8,64,512]{2,1,0:T(8,128)(2,1)S(1)}, bf16[8,64,512]{2,1,0:T(8,128)(2,1)}, u32[]{:S(2)}) copy-start(bf16[8,64,512]{2,1,0:T(8,128)(2,1)} %copy-done.1) | copy-start | bytes 1572868
  84.7 187.3 %all-to-all-start = ((bf16[8,8,128,512]{3,2,1,0:T(8,128)(2,1)}), bf16[8,8,128,512]{3,2,1,0:T(8,128)(2,1)}, u32[]{:S(2)}, u32[]{:S(2)}) async-start(bf16[8,8,128,512]{3,2,1,0:T(8,128)(2,1)} %bitcast.109), calls=%async_computation | async-start | bytes 16777216 | tf_op jit(solution)/shard_map/all_to_all | solution.py:128
  90.0 3.4 copy-start.9
  97.6 5.1 %copy-start.7 = (bf16[2,512,256]{2,1,0:T(8,128)(2,1)S(1)}, bf16[2,512,256]{2,1,0:T(8,128)(2,1)}, u32[]{:S(2)}) copy-start(bf16[2,512,256]{2,1,0:T(8,128)(2,1)} %param.14) | copy-start | bytes 1572868
  97.6 5.5 %copy-start.4 = (bf16[4,512,256]{2,1,0:T(8,128)(2,1)S(1)}, bf16[4,512,256]{2,1,0:T(8,128)(2,1)}, u32[]{:S(2)}) copy-start(bf16[4,512,256]{2,1,0:T(8,128)(2,1)} %param.13) | copy-start | bytes 3145732
  354.7 5.1 %copy-start.11 = (f32[8,512]{1,0:T(8,128)S(1)}, f32[8,512]{1,0:T(8,128)}, u32[]{:S(2)}) copy-start(f32[8,512]{1,0:T(8,128)} %broadcast_multiply_fusion.2) | copy-start | bytes 49156
  359.8 5.3 %copy-start.5 = (f32[4,128,256]{2,1,0:T(8,128)S(1)}, f32[4,128,256]{2,1,0:T(8,128)}, u32[]{:S(2)}) copy-start(f32[4,128,256]{2,1,0:T(8,128)} %pad_maximum_fusion.1) | copy-start | bytes 1572868
where the time goes:
time: 371 us; the launch traced here: 368 us
  waiting for transfers between devices  178 us (48%)
  local copies, waits for them, and re-layouts  81.3 us (22%)
  matrix products  58.4 us (16%)
  other arithmetic  37.6 us (10%)
  starting transfers between devices  12.5 us (3%)
    all_to_all x1, waiting for transfers between devices, on_device(): lax.all_to_all(leaf_buffer.reshape(peer_count, near_slots, FEAT + R, LEAF...  168 us
    dot_general x15, matrix products, tile_products(): jnp.einsum('gra,gab->grb', sources[:, FEAT:], kernel, preferred_element_t...  48.5 us
    scatter x1, local copies, waits for them, and re-layouts, on_device(): leaf_buffer = jnp.zeros((peer_count * near_slots, FEAT + R, LEAF), jnp.bf...  19.5 us
    squeeze x14, local copies, waits for them, and re-layouts, grouped_products(): lax.map(lambda couple: tile_products(couple[0], couple[1]), paired)  15.1 us
    reduce_sum x14, other arithmetic, kernel_tiles(): dst_sq = jnp.sum(dst_f * dst_f, axis=-2)  14.4 us
    all_to_all x1, waiting for transfers between devices, on_device(): lax.all_to_all(far_buffer.reshape(peer_count, far_slots, R, RANK), 'leaf'...  10.2 us
    scatter x1, local copies, waits for them, and re-layouts, on_device(): far_buffer = jnp.zeros((peer_count * far_slots, R, RANK), jnp.bfloat16).a...  9.79 us
    gather x1, local copies, waits for them, and re-layouts, on_device(): leaf_arrived.reshape(peer_count * near_slots, FEAT + R, LEAF)[my_slots]  8.7 us
  transfers between devices with their start and end apart: 2, of which 2 were waited for; matrix products, arithmetic and copies ran while one was open for 14% of the time, Pallas kernels for 0%

commit v1 on v0

--- a/solution.py
+++ b/solution.py
@@ -1,6 +1,10 @@
+import functools
+
 import jax
 import jax.numpy as jnp
 from jax import lax
+from jax.experimental import pallas as pl
+from jax.experimental.pallas import tpu as pltpu
 from jax.sharding import PartitionSpec as P
 
 FEAT = 64
@@ -66,7 +70,7 @@
     return child_far + spread
 
 
-def on_device(coords, rhs, basis, transfer_one, transfer_two, far_blocks, neighbours, far_lists):
+def exchanged(coords, rhs, basis, transfer_one, transfer_two, far_blocks, neighbours, far_lists):
     peer_count = lax.axis_size("leaf")
     device_index = lax.axis_index("leaf")
     local_leaves = basis.shape[0]
@@ -148,6 +152,147 @@
     return result.transpose(1, 0, 2).reshape(R, local_leaves * LEAF)
 
 
+def near_kernel(list_ref, *refs):
+    sources, charges = refs[:NB], refs[NB : 2 * NB]
+    target_ref, out_ref = refs[2 * NB], refs[2 * NB + 1]
+    target = target_ref[...]
+    target_f = target.astype(jnp.float32)
+    target_half = 0.5 * jnp.sum(target_f * target_f, axis=0, keepdims=True)
+    total = None
+    for source_ref, charge_ref in zip(sources, charges):
+        source = source_ref[...]
+        source_f = source.astype(jnp.float32)
+        source_half = 0.5 * jnp.sum(source_f * source_f, axis=0, keepdims=True)
+        inner = lax.dot_general(
+            source, target, (((0,), (0,)), ((), ())), preferred_element_type=jnp.float32
+        )
+        kernel = jnp.exp(inner - source_half.T - target_half).astype(jnp.bfloat16)
+        term = jnp.dot(charge_ref[...], kernel, preferred_element_type=jnp.float32)
+        total = term if total is None else total + term
+    out_ref[...] = total
+
+
+def near_products(listed, all_coords, all_rhs, coords):
+    local_leaves = listed.shape[0]
+    per_device = all_rhs.shape[2] // LEAF
+
+    def picked(slot):
+        def index(leaf, list_ref):
+            chosen = list_ref[leaf, slot]
+            return (chosen // per_device, 0, chosen % per_device)
+
+        return index
+
+    return pl.pallas_call(
+        near_kernel,
+        grid_spec=pltpu.PrefetchScalarGridSpec(
+            num_scalar_prefetch=1,
+            grid=(local_leaves,),
+            in_specs=[pl.BlockSpec((None, FEAT, LEAF), picked(slot)) for slot in range(NB)]
+            + [pl.BlockSpec((None, R, LEAF), picked(slot)) for slot in range(NB)]
+            + [pl.BlockSpec((FEAT, LEAF), lambda leaf, list_ref: (0, leaf))],
+            out_specs=pl.BlockSpec((R, LEAF), lambda leaf, list_ref: (0, leaf)),
+        ),
+        out_shape=jax.ShapeDtypeStruct((R, local_leaves * LEAF), jnp.float32),
+        compiler_params=pltpu.CompilerParams(vmem_limit_bytes=32 * 1024 * 1024),
+        cost_estimate=pl.CostEstimate(
+            flops=local_leaves * NB * LEAF * LEAF * 1024,
+            bytes_accessed=local_leaves * NB * LEAF * 256,
+            transcendentals=local_leaves * NB * LEAF * LEAF,
+        ),
+        name="near",
+    )(listed, *[all_coords] * NB, *[all_rhs] * NB, coords)
+
+
+def far_kernel(list_ref, *refs):
+    weights = refs[:FAR]
+    block_ref, out_ref = refs[FAR], refs[FAR + 1]
+    total = None
+    for partner in range(FAR):
+        term = jnp.dot(
+            weights[partner][...], block_ref[partner], preferred_element_type=jnp.float32
+        )
+        total = term if total is None else total + term
+    out_ref[...] = total
+
+
+def far_products(listed, skeleton, far_blocks):
+    node_count = listed.shape[0]
+
+    def picked(partner):
+        return lambda node, list_ref: (list_ref[node, partner], 0, 0)
+
+    return pl.pallas_call(
+        far_kernel,
+        grid_spec=pltpu.PrefetchScalarGridSpec(
+            num_scalar_prefetch=1,
+            grid=(node_count,),
+            in_specs=[pl.BlockSpec((None, R, RANK), picked(partner)) for partner in range(FAR)]
+            + [pl.BlockSpec((None, FAR, RANK, RANK), lambda node, list_ref: (node, 0, 0, 0))],
+            out_specs=pl.BlockSpec((None, R, RANK), lambda node, list_ref: (node, 0, 0)),
+        ),
+        out_shape=jax.ShapeDtypeStruct((node_count, R, RANK), jnp.float32),
+        compiler_params=pltpu.CompilerParams(vmem_limit_bytes=32 * 1024 * 1024),
+        cost_estimate=pl.CostEstimate(
+            flops=node_count * FAR * 2 * R * RANK * RANK,
+            bytes_accessed=node_count * FAR * (RANK + R) * RANK * 2,
+            transcendentals=0,
+        ),
+        name="far",
+    )(listed, *[skeleton] * FAR, far_blocks)
+
+
+def on_device(coords, rhs, basis, transfer_one, transfer_two, far_blocks, neighbours, far_lists):
+    peer_count = lax.axis_size("leaf")
+    local_leaves = basis.shape[0]
+    if (NB - 1) * local_leaves < (peer_count - 1) * local_leaves:
+        return exchanged(
+            coords, rhs, basis, transfer_one, transfer_two, far_blocks, neighbours, far_lists
+        )
+    return gathered(
+        coords, rhs, basis, transfer_one, transfer_two, far_blocks, neighbours, far_lists
+    )
+
+
+def gathered(coords, rhs, basis, transfer_one, transfer_two, far_blocks, neighbours, far_lists):
+    peer_count = lax.axis_size("leaf")
+    parts = lax.axis_size("rhs")
+    device_index = lax.axis_index("leaf")
+    local_leaves = basis.shape[0]
+    node_count = far_blocks.shape[0]
+    columns = rhs.shape[1]
+    all_rhs = lax.all_gather(rhs, "leaf")
+    share = lax.dynamic_slice_in_dim(
+        coords, lax.axis_index("rhs") * (FEAT // parts), FEAT // parts, 0
+    )
+    all_coords = lax.all_gather(share, ("leaf", "rhs")).reshape(peer_count, FEAT, columns)
+    charges = rhs.reshape(R, local_leaves, LEAF).transpose(1, 0, 2)
+    skel_zero = jnp.einsum(
+        "lra,lak->lrk", charges, basis, preferred_element_type=jnp.float32
+    ).astype(jnp.bfloat16)
+    skel_one = jnp.einsum(
+        "mrj,mjk->mrk", join_pairs(skel_zero), transfer_one, preferred_element_type=jnp.float32
+    ).astype(jnp.bfloat16)
+    skel_two = jnp.einsum(
+        "mrj,mjk->mrk", join_pairs(skel_one), transfer_two, preferred_element_type=jnp.float32
+    ).astype(jnp.bfloat16)
+    skeleton = jnp.concatenate([skel_zero, skel_one, skel_two], axis=0)
+    all_skeleton = lax.all_gather(skeleton, "leaf").reshape(peer_count * node_count, R, RANK)
+    my_neighbours = lax.dynamic_slice_in_dim(neighbours, device_index * local_leaves, local_leaves, 0)
+    my_far = lax.dynamic_slice_in_dim(far_lists, device_index * node_count, node_count, 0)
+    near = near_products(my_neighbours, all_coords, all_rhs, coords)
+    far = far_products(my_far, all_skeleton, far_blocks)
+    far_zero = far[:local_leaves]
+    far_one = far[local_leaves : local_leaves * 3 // 2]
+    far_two = far[local_leaves * 3 // 2 :]
+    middle = descend(far_two, transfer_two, far_one)
+    lowest = descend(middle, transfer_one, far_zero)
+    spread = jnp.einsum(
+        "lrk,lak->lra", lowest.astype(jnp.bfloat16), basis, preferred_element_type=jnp.float32
+    )
+    return near + spread.transpose(1, 0, 2).reshape(R, local_leaves * LEAF)
+
+
 def solution(mesh):
     return jax.shard_map(
         on_device,

time: 371 us -> 260 us (0.70)
  local copies, waits for them, and re-layouts: 81.3 us -> 14.2 us
  matrix products: 58.4 us -> 3.55 us
  other arithmetic: 37.6 us -> 1.96 us
  Pallas kernels: 0 us -> 34.9 us
  waiting for transfers between devices: 178 us -> 192 us
  between operations: 0.35 us -> 13.3 us
  starting transfers between devices: 12.5 us -> 0.08 us
    all_gather x0 -> x3, waiting for transfers between devices: none -> 191 us  [the longest x1 67.2 us: gathered(): lax.all_gather(skeleton, 'leaf').reshape(peer_count * node_count, R, RANK)]
    all_to_all x2 -> x0, waiting for transfers between devices: 178 us -> none  [the longest x1 168 us: on_device(): lax.all_to_all(leaf_buffer.reshape(peer_count, near_slots, FEAT + R, LEAF...]
    dot_general x20 -> x4, matrix products: 57.7 us -> 2.83 us  [the longest x1 1.55 us: gathered(): jnp.einsum('lra,lak->lrk', charges, basis, preferred_element_type=jnp.flo...]
    pallas_call x0 -> x2, Pallas kernels: none -> 34.9 us  [the longest x1 31.1 us: near_products(): pl.pallas_call(near_kernel, grid_spec=pltpu.PrefetchScalarGridSpec(num_sc...]
    scatter x2 -> x0, local copies, waits for them, and re-layouts: 29.3 us -> none  [the longest x1 19.5 us: on_device(): leaf_buffer = jnp.zeros((peer_count * near_slots, FEAT + R, LEAF), jnp.bf...]
    gather x12 -> x0, local copies, waits for them, and re-layouts: 25.6 us -> none  [the longest x1 8.7 us: on_device(): leaf_arrived.reshape(peer_count * near_slots, FEAT + R, LEAF)[my_slots]]
    reduce_sum x33 -> x0, other arithmetic: 23.2 us -> none  [the longest x14 14.4 us: kernel_tiles(): dst_sq = jnp.sum(dst_f * dst_f, axis=-2)]
    squeeze x14 -> x0, local copies, waits for them, and re-layouts: 15.1 us -> none  [grouped_products(): lax.map(lambda couple: tile_products(couple[0], couple[1]), paired)]
  transfers between devices with their start and end apart: 2 -> 3, of which waited for: 2 -> 3; matrix products, arithmetic and copies ran while one was open for 14% -> 1% of each run, Pallas kernels for 0% -> 1%
where the time goes in v1:
time: 260 us
  waiting for transfers between devices  192 us (74%)
  Pallas kernels  34.9 us (13%)
  local copies, waits for them, and re-layouts  14.2 us (5%)
  between operations  13.3 us (5%)
  matrix products  3.55 us (1%)
    all_gather x1, waiting for transfers between devices, gathered(): lax.all_gather(skeleton, 'leaf').reshape(peer_count * node_count, R, RANK)  67.2 us
    all_gather x1, waiting for transfers between devices, gathered(): lax.all_gather(share, ('leaf', 'rhs')).reshape(peer_count, FEAT, columns)  63.1 us
    all_gather x1, waiting for transfers between devices, gathered(): all_rhs = lax.all_gather(rhs, 'leaf')  61.2 us
    pallas_call x1, Pallas kernels, near_products(): pl.pallas_call(near_kernel, grid_spec=pltpu.PrefetchScalarGridSpec(num_sc...  31.1 us
    unnamed x26, local copies, waits for them, and re-layouts  12.2 us
  transfers between devices with their start and end apart: 3, of which 3 were waited for; matrix products, arithmetic and copies ran while one was open for 1% of the time, Pallas kernels for 1%

profile of v1, /device:TPU:0, one launch (start us, length us, event | category | flops | bytes accessed | tf_op | source)
XLA Modules:
  0.0 260.1 jit_solution(9123746899229437766)
XLA Ops:
  6.5 0.0 copy-start
  6.5 0.0 all-gather.11.cloned.1.call-start
  6.5 0.0 copy-start.7
  6.5 1.6 copy-done
  8.1 0.0 copy-start.9
  8.1 1.6 convolution_convert_fusion
  9.7 0.0 copy-done.7
  9.7 0.0 copy-start.5
  9.7 0.0 copy-start.10
  9.8 0.0 copy-start.11
  9.8 0.3 convolution_convert_fusion.1
  10.1 0.0 copy-done.9
  10.1 0.2 convolution_convert_fusion.2
  10.3 0.8 pad_maximum_fusion.1
  11.1 0.0 all-gather.11.cloned.1.call-update
  11.2 0.0 all-gather.9.cloned.1.call-start
  11.2 0.7 all-gather.9.cloned.1.call-update
  11.9 0.0 all-gather.7.cloned.1.call-start
  12.0 0.0 copy-done.5
  12.0 0.7 constant_dynamic-slice_fusion.1
  12.7 0.0 all-gather.7.cloned.1.call-update
  12.7 0.0 copy-done.10
  12.7 0.1 constant_dynamic-slice_fusion.2
  12.8 0.1 copy.21.list_ref
  12.9 0.0 copy-done.11
  12.9 0.1 constant_dynamic-slice_fusion
  12.9 0.1 copy.22.list_ref
  13.0 67.2 %all-gather.11.cloned.1.call-done.refs_0_.refs_1_.refs_2_.refs_3_ = bf16[112,64,256]{2,1,0:T(8,128)(2,1)} async-done(((bf16[14,64,256]{2,1,0:T(8,128)(2,1)}), bf16[112,64,256]{2,1,0:T(8,128)(2,1)}) %all-gather.11.cloned.1.call-update) | async-done | bytes 3670032 | tf_op jit(solution)/shard_map/all_gather | solution.py:280
  80.3 2.0 copy-done.3
  82.3 0.0 copy-start.4
  82.3 3.1 %copy-done.4 = bf16[14,4,256,256]{3,2,1,0:T(8,128)(2,1)S(1)} copy-done((bf16[14,4,256,256]{3,2,1,0:T(8,128)(2,1)S(1)}, bf16[14,4,256,256]{3,2,1,0:T(8,128)(2,1)}, u32[]{:S(2)}) %copy-start.4) | copy-done | bytes 7340056
  85.4 3.8 %far.1 = f32[14,64,256]{2,1,0:T(8,128)S(1)} custom-call(s32[14,4]{1,0:T(8,128)S(1)} %copy.22.list_ref, bf16[112,64,256]{2,1,0:T(8,128)(2,1)S(1)} %copy-done.3, bf16[112,64,256]{2,1,0:T(8,128)(2,1)S(1)} %copy-done.3, bf16[112,64,256]{2,1,0:T(8,128)(2,1)S(1)} %copy-done.3, bf16[112,64,256]{2,1,0:T(8,128)(2,1)S(1)} %copy-done.3, ...), custom_call_target="tpu_custom_call" | custom-call | flops 469762048 | bytes 9175040 | tf_op jit(solution)/shard_map/far/pallas_call | solution.py:225
  89.1 0.0 copy-start.8
  89.1 0.3 fusion.2
  89.5 0.9 copy-done.8
  90.4 0.4 fusion.6
  90.8 0.1 fusion.8
  90.9 0.8 convolution_bitcast_fusion
  91.7 1.0 copy.26
  92.7 61.2 %all-gather.9.cloned.1.call-done = bf16[512,4096]{1,0:T(8,128)(2,1)} async-done(((bf16[64,4096]{1,0:T(8,128)(2,1)}), bf16[512,4096]{1,0:T(8,128)(2,1)}) %all-gather.9.cloned.1.call-update) | async-done | bytes 4194320 | tf_op jit(solution)/shard_map/all_gather | solution.py:264
  153.9 63.1 %all-gather.7.cloned.1.call-done = bf16[512,4096]{1,0:T(8,128)(2,1)} async-done(((bf16[16,4096]{1,0:T(8,128)(2,1)}), bf16[512,4096]{1,0:T(8,128)(2,1)}) %all-gather.7.cloned.1.call-update) | async-done | bytes 4194320 | tf_op jit(solution)/shard_map/all_gather | solution.py:268
  217.0 0.0 copy-start.1
  217.0 2.2 copy-done.1
  219.2 0.0 copy-start.2
  219.2 2.2 copy-done.2
  221.4 31.1 %near.1 = f32[64,4096]{1,0:T(8,128)S(1)} custom-call(s32[8,8]{1,0:T(8,128)S(1)} %copy.21.list_ref, bf16[8,64,4096]{2,1,0:T(8,128)(2,1)S(1)} %bitcast.41, bf16[8,64,4096]{2,1,0:T(8,128)(2,1)S(1)} %bitcast.42, bf16[8,64,4096]{2,1,0:T(8,128)(2,1)S(1)} %bitcast.43, bf16[8,64,4096]{2,1,0:T(8,128)(2,1)S(1)} %bitcast.44, bf16[8,64,4096]{2,1,0:T(8,128)(2,1)S(1)} %bitcast.45, ...), custom_call_target="tpu_custom_call" | custom-call | flops 17179869184 | bytes 8388608 | tf_op jit(solution)/shard_map/near/pallas_call | solution.py:186
  252.5 0.0 copy-done.6
  252.5 1.1 add.23
  (7 shorter events, 0.1 us)
Async XLA Ops:
  6.5 1.6 copy-start
  6.5 73.7 %all-gather.11.cloned.1.call-start = ((), (), s32[]{:S(2)}) async-start(), calls=%async_computation.2 | async-start | bytes 4128768 | tf_op jit(solution)/shard_map/all_gather | solution.py:280
  6.5 3.2 %copy-start.7 = (bf16[4,512,256]{2,1,0:T(8,128)(2,1)S(1)}, bf16[4,512,256]{2,1,0:T(8,128)(2,1)}, u32[]{:S(2)}) copy-start(bf16[4,512,256]{2,1,0:T(8,128)(2,1)} %param.11) | copy-start | bytes 3145732
  8.1 2.0 copy-start.9
  9.7 2.2 copy-start.5
  9.7 3.0 %copy-start.10 = (s32[64,8]{0,1:T(8,128)S(1)}, s32[64,8]{0,1:T(8,128)}, u32[]{:S(2)}) copy-start(s32[64,8]{0,1:T(8,128)} %param.14) | copy-start | bytes 6148
  9.8 3.1 %copy-start.11 = (s32[112,4]{0,1:T(4,128)S(1)}, s32[112,4]{0,1:T(4,128)}, u32[]{:S(2)}) copy-start(s32[112,4]{0,1:T(4,128)} %param.15) | copy-start | bytes 5380
  11.2 142.7 %all-gather.9.cloned.1.call-start = ((), (), s32[]{:S(2)}) async-start(), calls=%async_computation.1 | async-start | bytes 4718592 | tf_op jit(solution)/shard_map/all_gather | solution.py:264
  11.9 205.1 %all-gather.7.cloned.1.call-start = ((), (), s32[]{:S(2)}) async-start(), calls=%async_computation | async-start | bytes 4325376 | tf_op jit(solution)/shard_map/all_gather | solution.py:268
  80.3 2.0 copy-start.3
  82.3 3.1 %copy-start.4 = (bf16[14,4,256,256]{3,2,1,0:T(8,128)(2,1)S(1)}, bf16[14,4,256,256]{3,2,1,0:T(8,128)(2,1)}, u32[]{:S(2)}) copy-start(bf16[14,4,256,256]{3,2,1,0:T(8,128)(2,1)} %refs_4_.1) | copy-start | bytes 22020100
  89.1 1.3 copy-start.8
  217.0 2.2 copy-start.1
  219.2 2.2 copy-start.2
  221.4 31.2 %copy-start.6 = (f32[8,8,8,512]{3,2,0,1:T(8,128)S(1)}, f32[8,8,8,512]{3,2,0,1:T(8,128)}, u32[]{:S(2)}) copy-start(f32[8,8,8,512]{3,2,0,1:T(8,128)} %copy.26) | copy-start | bytes 3145732
Sparse Core Ops, SparseCore 0:
  11.3 68.9 all-gather.10
  82.4 71.4 all-gather.8
  156.8 60.1 all-gather.6

commit v2 on v0

--- a/solution.py
+++ b/solution.py
@@ -1,6 +1,10 @@
+import functools
+
 import jax
 import jax.numpy as jnp
 from jax import lax
+from jax.experimental import pallas as pl
+from jax.experimental.pallas import tpu as pltpu
 from jax.sharding import PartitionSpec as P
 
 FEAT = 64
@@ -66,7 +70,7 @@
     return child_far + spread
 
 
-def on_device(coords, rhs, basis, transfer_one, transfer_two, far_blocks, neighbours, far_lists):
+def exchanged(coords, rhs, basis, transfer_one, transfer_two, far_blocks, neighbours, far_lists):
     peer_count = lax.axis_size("leaf")
     device_index = lax.axis_index("leaf")
     local_leaves = basis.shape[0]
@@ -146,6 +150,325 @@
         "lrk,lak->lra", lowest.astype(jnp.bfloat16), basis, preferred_element_type=jnp.float32
     )
     return result.transpose(1, 0, 2).reshape(R, local_leaves * LEAF)
+
+
+POINT, SKEL, CHARGE = 0, 1, 2
+
+
+def visit_orders(rows):
+    return [sorted(range(rows), key=lambda row: (abs(row - at), row)) for at in range(rows)]
+
+
+def tile(source, target, target_half, charge):
+    source_f = source.astype(jnp.float32)
+    source_half = 0.5 * jnp.sum(source_f * source_f, axis=0, keepdims=True)
+    inner = lax.dot_general(
+        source, target, (((0,), (0,)), ((), ())), preferred_element_type=jnp.float32
+    )
+    kernel = jnp.exp(inner - source_half.T - target_half).astype(jnp.bfloat16)
+    return jnp.dot(charge, kernel, preferred_element_type=jnp.float32)
+
+
+def half_square(points):
+    points_f = points.astype(jnp.float32)
+    return 0.5 * jnp.sum(points_f * points_f, axis=0, keepdims=True)
+
+
+def whole_kernel(
+    rows, parts, source_tab, target_tab, place_tab, far_tab, coords, rhs, skeleton, basis_hbm,
+    one_hbm, two_hbm, blocks_hbm, out, *scratch
+):
+    slots = 2 * rows
+    points_at = (None,) + scratch[: slots - 1]
+    charges_at = (None,) + scratch[slots - 1 : 2 * slots - 2]
+    (
+        skel_at, terms, far_at, basis, one, two, blocks, local_sem, send_sem, recv_sem,
+        peer_send_sem, peer_recv_sem,
+    ) = scratch[2 * slots - 2 :]
+    orders = visit_orders(rows)
+    local_leaves, node_count = basis.shape[0], blocks.shape[0]
+    share = coords.shape[1] // parts
+    leaf = lax.axis_index("leaf")
+    row, side = leaf // 2, leaf % 2
+    part = lax.axis_index("rhs")
+    across = (row * 2 + 1 - side, part)
+
+    loads = [
+        pltpu.make_async_copy(source, target, local_sem.at[which])
+        for which, (source, target) in enumerate(
+            ((blocks_hbm, blocks), (basis_hbm, basis), (one_hbm, one), (two_hbm, two))
+        )
+    ]
+    for load in loads:
+        load.start()
+
+    barrier = pltpu.get_barrier_semaphore()
+    mesh_ids = pl.DeviceIdType.MESH
+    partners = [across] + [(leaf, (part + away) % parts) for away in range(1, parts)]
+    for partner in partners:
+        pl.semaphore_signal(barrier, inc=1, device_id=partner, device_id_type=mesh_ids)
+
+    @pl.when(row > 0)
+    def _():
+        pl.semaphore_signal(barrier, inc=1, device_id=(leaf - 2, part), device_id_type=mesh_ids)
+
+    @pl.when(row < rows - 1)
+    def _():
+        pl.semaphore_signal(barrier, inc=1, device_id=(leaf + 2, part), device_id_type=mesh_ids)
+
+    ahead = (row + rows - 1) // rows + (2 * rows - 2 - row) // rows
+    pl.semaphore_wait(barrier, len(partners) + ahead)
+
+    def mine(points):
+        return points.at[:, pl.ds(pl.multiple_of(part * share, share), share), :]
+
+    def held(kind, slot, own):
+        if kind == POINT:
+            if own and slot == 0:
+                return mine(coords)
+            return mine(points_at[slot])
+        if kind == SKEL:
+            if own and slot == 0:
+                return skeleton
+            return skel_at.at[pl.ds((slot - 1) * node_count, node_count)]
+        return rhs if own and slot == 0 else charges_at[slot]
+
+    def remote(kind, slot, way, to_slot, device):
+        return pltpu.make_async_remote_copy(
+            src_ref=held(kind, slot, True),
+            dst_ref=held(kind, to_slot, False),
+            send_sem=send_sem.at[kind, slot, way],
+            recv_sem=recv_sem.at[kind, to_slot],
+            device_id=device,
+            device_id_type=mesh_ids,
+        )
+
+    def to_peer(slot, away):
+        return pltpu.make_async_remote_copy(
+            src_ref=mine(points_at[slot]),
+            dst_ref=mine(points_at[slot]),
+            send_sem=peer_send_sem.at[slot, away - 1],
+            recv_sem=peer_recv_sem.at[slot, away - 1],
+            device_id=(leaf, (part + away) % parts),
+            device_id_type=mesh_ids,
+        )
+
+    def sends(at, kind, slot):
+        beside, rank = divmod(slot, rows)
+        origin = orders[at][rank]
+        found = []
+        if kind == POINT or beside == 0:
+            if origin <= at < rows - 1:
+                to_slot = beside * rows + orders[at + 1].index(origin)
+                found.append(remote(kind, slot, 0, to_slot, (leaf + 2, part)))
+            if origin >= at > 0:
+                to_slot = beside * rows + orders[at - 1].index(origin)
+                found.append(remote(kind, slot, 1, to_slot, (leaf - 2, part)))
+        if (beside == 0 and kind != POINT) or slot == 0:
+            found.append(remote(kind, slot, 2, rows + rank, across))
+        if kind == POINT and slot > 0:
+            found.extend(to_peer(slot, away) for away in range(1, parts))
+        return found
+
+    def arrived(kind, slot):
+        remote(kind, slot, 2, slot, across).wait_recv()
+
+    def pass_on(at, kind, slot):
+        arrived(kind, slot)
+        for copy in sends(at, kind, slot):
+            copy.start()
+
+    def phase(at, distance):
+        if distance == 0:
+            for kind in (POINT, SKEL, CHARGE):
+                for copy in sends(at, kind, 0):
+                    copy.start()
+            return
+        if distance == 1:
+            pass_on(at, POINT, rows)
+        ranks = [rank for rank in range(rows) if abs(orders[at][rank] - at) == distance]
+        for kind in (POINT, SKEL, CHARGE):
+            for rank in ranks:
+                pass_on(at, kind, rank)
+        for rank in ranks:
+            pass_on(at, POINT, rows + rank)
+
+    def by_row(action):
+        for at in range(rows):
+            pl.when(row == at)(functools.partial(action, at))
+
+    def tiles(slot):
+        for away in range(1, parts):
+            to_peer(slot, away).wait_recv()
+        if slot >= rows:
+            arrived(CHARGE, slot)
+        first = (slot - 1) * local_leaves
+
+        def entry(index, carry):
+            where = first + index
+            source = points_at[slot][source_tab[where]]
+            target = coords[target_tab[where]]
+            charge = charges_at[slot][source_tab[where]]
+            terms[where] = tile(source, target, half_square(target), charge)
+            return carry
+
+        lax.fori_loop(0, local_leaves, entry, 0, unroll=UNROLL)
+
+    by_row(functools.partial(phase, distance=0))
+
+    own_first = (slots - 1) * local_leaves
+
+    def own_entry(index, carry):
+        target = coords[index]
+        terms[own_first + index] = tile(target, target, half_square(target), rhs[index])
+        return carry
+
+    lax.fori_loop(0, local_leaves, own_entry, 0, unroll=UNROLL)
+    for distance in range(1, rows):
+        by_row(functools.partial(phase, distance=distance))
+        tiles(distance)
+        tiles(rows + distance - 1)
+
+    for load in loads:
+        load.wait()
+    for slot in range(rows, slots):
+        arrived(SKEL, slot)
+
+    def far_node(node, carry):
+        total = None
+        for partner in range(FAR):
+            weights = skel_at[far_tab[node * FAR + partner]]
+            term = jnp.dot(weights, blocks[node, partner], preferred_element_type=jnp.float32)
+            total = term if total is None else total + term
+        far_at[node] = total
+        return carry
+
+    lax.fori_loop(0, node_count, far_node, 0, unroll=2)
+
+    def spread_to(parent, transfer):
+        return lax.dot_general(
+            parent.astype(jnp.bfloat16), transfer, (((1,), (1,)), ((), ())),
+            preferred_element_type=jnp.float32,
+        )
+
+    first_one, first_two = local_leaves, local_leaves * 3 // 2
+    for parent in range(node_count - first_two):
+        spread = spread_to(far_at[first_two + parent], two[parent])
+        for child in range(2):
+            far_at[first_one + 2 * parent + child] += spread[:, child * RANK : (child + 1) * RANK]
+    for parent in range(first_two - first_one):
+        spread = spread_to(far_at[first_one + parent], one[parent])
+        for child in range(2):
+            far_at[2 * parent + child] += spread[:, child * RANK : (child + 1) * RANK]
+
+    tiles(slots - 1)
+
+    for index in range(local_leaves):
+        total = terms[own_first + index]
+        for listed in range(NB - 1):
+            total = total + terms[place_tab[index * (NB - 1) + listed]]
+        out[:, index * LEAF : (index + 1) * LEAF] = total + spread_to(far_at[index], basis[index])
+
+    def finish(at):
+        for kind in (POINT, SKEL, CHARGE):
+            for slot in range(slots):
+                for copy in sends(at, kind, slot):
+                    copy.wait_send()
+
+    by_row(finish)
+
+
+UNROLL = 2
+
+
+def on_device(coords, rhs, basis, transfer_one, transfer_two, far_blocks, neighbours, far_lists):
+    peer_count = lax.axis_size("leaf")
+    whole_lists = peer_count == NB and peer_count % 2 == 0
+    route = gathered if whole_lists and FEAT % lax.axis_size("rhs") == 0 else exchanged
+    return route(coords, rhs, basis, transfer_one, transfer_two, far_blocks, neighbours, far_lists)
+
+
+def gathered(coords, rhs, basis, transfer_one, transfer_two, far_blocks, neighbours, far_lists):
+    peer_count = lax.axis_size("leaf")
+    parts = lax.axis_size("rhs")
+    rows = peer_count // 2
+    device_index = lax.axis_index("leaf")
+    local_leaves = basis.shape[0]
+    node_count = far_blocks.shape[0]
+    width = rhs.shape[1]
+    remote_count = (NB - 1) * local_leaves
+    points = coords.reshape(FEAT, local_leaves, LEAF).transpose(1, 0, 2)
+    charges = rhs.reshape(R, local_leaves, LEAF).transpose(1, 0, 2)
+    skel_zero = jnp.einsum(
+        "lra,lak->lrk", charges, basis, preferred_element_type=jnp.float32
+    ).astype(jnp.bfloat16)
+    skel_one = jnp.einsum(
+        "mrj,mjk->mrk", join_pairs(skel_zero), transfer_one, preferred_element_type=jnp.float32
+    ).astype(jnp.bfloat16)
+    skel_two = jnp.einsum(
+        "mrj,mjk->mrk", join_pairs(skel_one), transfer_two, preferred_element_type=jnp.float32
+    ).astype(jnp.bfloat16)
+    skeleton = jnp.concatenate([skel_zero, skel_one, skel_two], axis=0)
+
+    orders = visit_orders(rows)
+    row, side = device_index // 2, device_index % 2
+
+    def slot_of(owner):
+        origin, beside = owner // 2, (owner % 2 + side) % 2
+        rank = jnp.zeros_like(owner)
+        for at in range(rows):
+            for place in range(rows):
+                matches = jnp.logical_and(row == at, origin == orders[at][place])
+                rank = jnp.where(matches, place, rank)
+        return beside * rows + rank
+
+    listed = lax.dynamic_slice_in_dim(neighbours, device_index * local_leaves, local_leaves, 0)
+    remote = listed[:, 1:].reshape(remote_count)
+    slot = slot_of(remote // local_leaves)
+    position = jnp.arange(remote_count, dtype=jnp.int32)
+    earlier = jnp.logical_and(slot[:, None] == slot[None, :], position[None, :] < position[:, None])
+    place_tab = (slot - 1) * local_leaves + jnp.sum(earlier, axis=1, dtype=jnp.int32)
+    chosen = place_tab[None, :] == position[:, None]
+    source_tab = jnp.sum(jnp.where(chosen, (remote % local_leaves)[None, :], 0), axis=1)
+    target_tab = jnp.sum(jnp.where(chosen, (position // (NB - 1))[None, :], 0), axis=1)
+    far_listed = lax.dynamic_slice_in_dim(far_lists, device_index * node_count, node_count, 0)
+    far_listed = far_listed.reshape(node_count * FAR)
+    far_tab = (slot_of(far_listed // node_count) - 1) * node_count + far_listed % node_count
+
+    smem = pl.BlockSpec(memory_space=pltpu.SMEM)
+    vmem = pl.BlockSpec(memory_space=pltpu.VMEM)
+    anywhere = pl.BlockSpec(memory_space=pl.ANY)
+    remote_slots = peer_count - 1
+    bf16 = jnp.bfloat16
+    return pl.pallas_call(
+        functools.partial(whole_kernel, rows, parts),
+        out_shape=jax.ShapeDtypeStruct((R, width), jnp.float32),
+        in_specs=[smem] * 4 + [vmem] * 3 + [anywhere] * 4,
+        out_specs=vmem,
+        scratch_shapes=[pltpu.VMEM((local_leaves, FEAT, LEAF), bf16)] * remote_slots
+        + [pltpu.VMEM((local_leaves, R, LEAF), bf16)] * remote_slots
+        + [
+            pltpu.VMEM((remote_slots * node_count, R, RANK), bf16),
+            pltpu.VMEM((peer_count * local_leaves, R, LEAF), jnp.float32),
+            pltpu.VMEM((node_count, R, RANK), jnp.float32),
+            pltpu.VMEM(basis.shape, bf16),
+            pltpu.VMEM(transfer_one.shape, bf16),
+            pltpu.VMEM(transfer_two.shape, bf16),
+            pltpu.VMEM(far_blocks.shape, bf16),
+            pltpu.SemaphoreType.DMA((4,)),
+            pltpu.SemaphoreType.DMA((3, peer_count, 3)),
+            pltpu.SemaphoreType.DMA((3, peer_count)),
+            pltpu.SemaphoreType.DMA((peer_count, parts - 1)),
+            pltpu.SemaphoreType.DMA((peer_count, parts - 1)),
+        ],
+        compiler_params=pltpu.CompilerParams(
+            collective_id=0, has_side_effects=True, vmem_limit_bytes=56 * 1024 * 1024
+        ),
+        name="whole",
+    )(
+        source_tab, target_tab, place_tab, far_tab, points, charges, skeleton, basis, transfer_one,
+        transfer_two, far_blocks,
+    )
 
 
 def solution(mesh):

time: 371 us -> 116 us (0.31)
  waiting for transfers between devices: 178 us -> 0 us
  Pallas kernels: 0 us -> 105 us
  local copies, waits for them, and re-layouts: 81.3 us -> 4.24 us
  matrix products: 58.4 us -> 2.77 us
  other arithmetic: 37.6 us -> 3.95 us
  starting transfers between devices: 12.5 us -> 0 us
    all_to_all x2 -> x0, waiting for transfers between devices: 178 us -> none  [the longest x1 168 us: on_device(): lax.all_to_all(leaf_buffer.reshape(peer_count, near_slots, FEAT + R, LEAF...]
    pallas_call x0 -> x1, Pallas kernels: none -> 105 us  [gathered(): pl.pallas_call(functools.partial(whole_kernel, rows, parts), out_shape=ja...]
    dot_general x22 -> x3, matrix products: 58.4 us -> 2.77 us  [the longest x1 2.26 us: gathered(): jnp.einsum('lra,lak->lrk', charges, basis, preferred_element_type=jnp.flo...]
    scatter x2 -> x0, local copies, waits for them, and re-layouts: 29.3 us -> none  [the longest x1 19.5 us: on_device(): leaf_buffer = jnp.zeros((peer_count * near_slots, FEAT + R, LEAF), jnp.bf...]
    gather x12 -> x0, local copies, waits for them, and re-layouts: 25.6 us -> none  [the longest x1 8.7 us: on_device(): leaf_arrived.reshape(peer_count * near_slots, FEAT + R, LEAF)[my_slots]]
    reduce_sum x33 -> x2, other arithmetic: 23.2 us -> 0.88 us  [the longest x1 0.7 us: gathered(): jnp.sum(jnp.where(chosen, (position // (NB - 1))[None, :], 0), axis=1)]
    squeeze x14 -> x0, local copies, waits for them, and re-layouts: 15.1 us -> none  [grouped_products(): lax.map(lambda couple: tile_products(couple[0], couple[1]), paired)]
    all_to_all x2 -> x0, starting transfers between devices: 12.5 us -> none  [the longest x1 7.25 us: on_device(): lax.all_to_all(far_buffer.reshape(peer_count, far_slots, R, RANK), 'leaf'...]
  transfers between devices with their start and end apart: 2 -> 0, of which waited for: 2 -> 0; matrix products, arithmetic and copies ran while one was open for 14% -> 0% of each run, Pallas kernels for 0% -> 0%
where the time goes in v2:
time: 116 us
  Pallas kernels  105 us (91%)
  local copies, waits for them, and re-layouts  4.24 us (4%)
  other arithmetic  3.95 us (3%)
  matrix products  2.77 us (2%)
    pallas_call x1, Pallas kernels, gathered(): pl.pallas_call(functools.partial(whole_kernel, rows, parts), out_shape=ja...  105 us

profile of v2, /device:TPU:0, one launch (start us, length us, event | category | flops | bytes accessed | tf_op | source)
XLA Modules:
  0.0 115.7 jit_solution(12590156254076670385)
XLA Ops:
  0.0 0.0 copy-start
  0.0 0.0 copy-start.1
  0.0 0.8 sign_compare_fusion
  0.9 0.1 copy.24
  1.0 0.1 ne.204
  1.1 0.0 copy-done
  1.1 0.1 constant_dynamic-slice_fusion
  1.2 0.1 copy.23
  1.2 0.1 reshape.281
  1.4 0.2 convert_reduce_fusion
  1.6 0.0 copy-start.5
  1.6 0.7 select_reduce_fusion
  2.3 0.8 dynamic-slice_divide_fusion
  3.0 0.1 copy.26
  3.1 0.1 div.63
  3.2 0.1 copy.25
  3.3 0.1 rem.160
  3.4 0.6 fusion.1.far_tab
  4.0 0.0 copy-start.2
  4.0 2.3 %convolution_convert_fusion = bf16[8,64,256]{2,1,0:T(8,128)(2,1)S(1)} fusion(bf16[8,512,256]{2,1,0:T(8,128)(2,1)} %basis_hbm.1, bf16[8,8,8,512]{3,2,1,0:T(8,128)(2,1)} %bitcast.28), kind=kOutput, calls=%fused_computation | convolution fusion | flops 134348800 | bytes 2883584 | tf_op jit(solution)/shard_map/lra,lak->lrk/dot_general | solution.py:402
  6.2 0.0 copy-start.3
  6.3 0.0 copy-start.4
  6.3 0.0 copy-done.1
  6.3 0.3 convolution_convert_fusion.1
  6.6 0.0 copy-done.5
  6.6 0.0 copy-done.2
  6.7 0.2 convolution_convert_fusion.2
  6.9 0.8 pad_maximum_fusion.skeleton
  7.7 0.0 copy-done.3
  7.7 0.0 copy-done.4
  7.7 1.1 bitcast_bitcast_fusion
  8.8 104.6 %whole.1 = f32[64,4096]{1,0:T(8,128)} custom-call(s32[56]{0:T(128)} %get-tuple-element.6.source_tab, s32[56]{0:T(128)} %get-tuple-element.5.target_tab, s32[56]{0:T(128)} %copy-done.5, s32[56]{0:T(128)} %fusion.1.far_tab, bf16[8,64,512]{2,1,0:T(8,128)(2,1)} %get-tuple-element.13.coords, bf16[8,64,512]{2,1,0:T(8,128)(2,1)} %get-tuple-element.12.rhs, ...), custom_call_target="tpu_custom_call" | custom-call | tf_op jit(solution)/shard_map/whole/pallas_call | solution.py:443
  113.4 2.3 %copy.39 = f32[64,4096]{1,0:T(8,128)} copy(f32[64,4096]{1,0:T(8,128)} %whole.1) | data formatting | bytes 2097152
  (5 shorter events, 0.1 us)
Async XLA Ops:
  0.0 1.1 copy-start
  0.0 6.3 %copy-start.1 = (bf16[4,512,256]{2,1,0:T(8,128)(2,1)S(1)}, bf16[4,512,256]{2,1,0:T(8,128)(2,1)}, u32[]{:S(2)}) copy-start(bf16[4,512,256]{2,1,0:T(8,128)(2,1)} %one_hbm.1) | copy-start | bytes 3145732
  1.6 5.1 %copy-start.5 = (s32[56]{0:T(128)}, s32[56]{0:T(128)S(1)}, u32[]{:S(2)}) copy-start(s32[56]{0:T(128)S(1)} %multiply_add_fusion.place_tab) | copy-start | bytes 676
  4.0 2.7 %copy-start.2 = (bf16[2,512,256]{2,1,0:T(8,128)(2,1)S(1)}, bf16[2,512,256]{2,1,0:T(8,128)(2,1)}, u32[]{:S(2)}) copy-start(bf16[2,512,256]{2,1,0:T(8,128)(2,1)} %two_hbm.1) | copy-start | bytes 1572868
  6.2 1.5 %copy-start.3 = (bf16[64,4096]{1,0:T(8,128)(2,1)S(1)}, bf16[64,4096]{1,0:T(8,128)(2,1)}, u32[]{:S(2)}) copy-start(bf16[64,4096]{1,0:T(8,128)(2,1)} %param.9) | copy-start | bytes 1572868
  6.3 1.5 %copy-start.4 = (bf16[64,4096]{1,0:T(8,128)(2,1)S(1)}, bf16[64,4096]{1,0:T(8,128)(2,1)}, u32[]{:S(2)}) copy-start(bf16[64,4096]{1,0:T(8,128)(2,1)} %param.8) | copy-start | bytes 1572868

commit v3 on v2

--- a/solution.py
+++ b/solution.py
@@ -152,7 +152,7 @@
     return result.transpose(1, 0, 2).reshape(R, local_leaves * LEAF)
 
 
-POINT, SKEL, CHARGE = 0, 1, 2
+POINT, EARLY, SKEL, LATE = 0, 1, 2, 3
 
 
 def visit_orders(rows):
@@ -175,16 +175,17 @@
 
 
 def whole_kernel(
-    rows, parts, source_tab, target_tab, place_tab, far_tab, coords, rhs, skeleton, basis_hbm,
+    rows, parts, source_tab, target_tab, place_tab, pick_tab, give_tab, far_tab, coords, rhs, basis_hbm,
     one_hbm, two_hbm, blocks_hbm, out, *scratch
 ):
     slots = 2 * rows
     points_at = (None,) + scratch[: slots - 1]
     charges_at = (None,) + scratch[slots - 1 : 2 * slots - 2]
+    skel_at = scratch[2 * slots - 2 : 2 * slots - 2 + rows]
     (
-        skel_at, terms, far_at, basis, one, two, blocks, local_sem, send_sem, recv_sem,
-        peer_send_sem, peer_recv_sem,
-    ) = scratch[2 * slots - 2 :]
+        given, partners_at, terms, far_at, basis, one, two, blocks, local_sem, send_sem,
+        recv_sem, peer_send_sem, peer_recv_sem,
+    ) = scratch[2 * slots - 2 + rows :]
     orders = visit_orders(rows)
     local_leaves, node_count = basis.shape[0], blocks.shape[0]
     share = coords.shape[1] // parts
@@ -196,7 +197,7 @@
     loads = [
         pltpu.make_async_copy(source, target, local_sem.at[which])
         for which, (source, target) in enumerate(
-            ((blocks_hbm, blocks), (basis_hbm, basis), (one_hbm, one), (two_hbm, two))
+            ((basis_hbm, basis), (one_hbm, one), (two_hbm, two), (blocks_hbm, blocks))
         )
     ]
     for load in loads:
@@ -222,21 +223,24 @@
     def mine(points):
         return points.at[:, pl.ds(pl.multiple_of(part * share, share), share), :]
 
-    def held(kind, slot, own):
+    def far_part(rank):
+        return pl.ds(rank * local_leaves, local_leaves)
+
+    def held(kind, slot, own, over):
         if kind == POINT:
-            if own and slot == 0:
-                return mine(coords)
-            return mine(points_at[slot])
+            return mine(coords if own and slot == 0 else points_at[slot])
         if kind == SKEL:
-            if own and slot == 0:
-                return skeleton
-            return skel_at.at[pl.ds((slot - 1) * node_count, node_count)]
-        return rhs if own and slot == 0 else charges_at[slot]
+            if over:
+                return given.at[far_part(slot)] if own else partners_at.at[far_part(slot - 1)]
+            return skel_at[slot]
+        half = local_leaves // 2
+        part_at = pl.ds(0, half) if kind == EARLY else pl.ds(half, local_leaves - half)
+        return (rhs if own and slot == 0 else charges_at[slot]).at[part_at]
 
     def remote(kind, slot, way, to_slot, device):
         return pltpu.make_async_remote_copy(
-            src_ref=held(kind, slot, True),
-            dst_ref=held(kind, to_slot, False),
+            src_ref=held(kind, slot, True, way == 2),
+            dst_ref=held(kind, to_slot, False, way == 2),
             send_sem=send_sem.at[kind, slot, way],
             recv_sem=recv_sem.at[kind, to_slot],
             device_id=device,
@@ -253,45 +257,73 @@
             device_id_type=mesh_ids,
         )
 
-    def sends(at, kind, slot):
-        beside, rank = divmod(slot, rows)
-        origin = orders[at][rank]
+    def along(at, kind, slot):
+        origin = orders[at][slot]
         found = []
-        if kind == POINT or beside == 0:
-            if origin <= at < rows - 1:
-                to_slot = beside * rows + orders[at + 1].index(origin)
-                found.append(remote(kind, slot, 0, to_slot, (leaf + 2, part)))
-            if origin >= at > 0:
-                to_slot = beside * rows + orders[at - 1].index(origin)
-                found.append(remote(kind, slot, 1, to_slot, (leaf - 2, part)))
-        if (beside == 0 and kind != POINT) or slot == 0:
-            found.append(remote(kind, slot, 2, rows + rank, across))
-        if kind == POINT and slot > 0:
-            found.extend(to_peer(slot, away) for away in range(1, parts))
+        if origin <= at < rows - 1:
+            to_slot = orders[at + 1].index(origin)
+            found.append(remote(kind, slot, 0, to_slot, (leaf + 2, part)))
+        if origin >= at > 0:
+            to_slot = orders[at - 1].index(origin)
+            found.append(remote(kind, slot, 1, to_slot, (leaf - 2, part)))
         return found
 
+    def beside(kind, slot):
+        return remote(kind, slot, 2, rows + slot, across)
+
     def arrived(kind, slot):
-        remote(kind, slot, 2, slot, across).wait_recv()
-
-    def pass_on(at, kind, slot):
-        arrived(kind, slot)
-        for copy in sends(at, kind, slot):
-            copy.start()
+        if slot < rows:
+            remote(kind, 0, 0, slot, across).wait_recv()
+        else:
+            remote(kind, slot - rows, 2, slot, across).wait_recv()
+
+    def share_points(slot):
+        for away in range(1, parts):
+            to_peer(slot, away).start()
+
+    def choose(rank):
+        def entry(index, carry):
+            place = rank * local_leaves + index
+            given[place] = skel_at[rank][give_tab[rows * local_leaves - local_leaves + place]]
+            if rank > 0:
+                taken = place - local_leaves
+                partners_at[taken] = skel_at[rank][pick_tab[taken]]
+            return carry
+
+        lax.fori_loop(0, local_leaves, entry, 0)
+
+    def start_along(kind, ranks, at):
+        for rank in ranks:
+            if at != orders[at][rank]:
+                arrived(kind, rank)
+            for copy in along(at, kind, rank):
+                copy.start()
+
+    def open_sends(at):
+        for kind in (POINT, EARLY):
+            start_along(kind, [0], at)
+            beside(kind, 0).start()
+
+    def more_sends(at):
+        for kind in (SKEL, LATE):
+            start_along(kind, [0], at)
+            beside(kind, 0).start()
 
     def phase(at, distance):
-        if distance == 0:
-            for kind in (POINT, SKEL, CHARGE):
-                for copy in sends(at, kind, 0):
-                    copy.start()
-            return
-        if distance == 1:
-            pass_on(at, POINT, rows)
         ranks = [rank for rank in range(rows) if abs(orders[at][rank] - at) == distance]
-        for kind in (POINT, SKEL, CHARGE):
+        for kind in (POINT, EARLY):
+            start_along(kind, ranks, at)
             for rank in ranks:
-                pass_on(at, kind, rank)
+                beside(kind, rank).start()
+                if kind == POINT:
+                    share_points(rank)
+        start_along(SKEL, ranks, at)
         for rank in ranks:
-            pass_on(at, POINT, rows + rank)
+            choose(rank)
+        start_along(LATE, ranks, at)
+        for rank in ranks:
+            beside(SKEL, rank).start()
+            beside(LATE, rank).start()
 
     def by_row(action):
         for at in range(rows):
@@ -301,7 +333,8 @@
         for away in range(1, parts):
             to_peer(slot, away).wait_recv()
         if slot >= rows:
-            arrived(CHARGE, slot)
+            arrived(EARLY, slot)
+            arrived(LATE, slot)
         first = (slot - 1) * local_leaves
 
         def entry(index, carry):
@@ -314,7 +347,7 @@
 
         lax.fori_loop(0, local_leaves, entry, 0, unroll=UNROLL)
 
-    by_row(functools.partial(phase, distance=0))
+    by_row(open_sends)
 
     own_first = (slots - 1) * local_leaves
 
@@ -323,21 +356,48 @@
         terms[own_first + index] = tile(target, target, half_square(target), rhs[index])
         return carry
 
-    lax.fori_loop(0, local_leaves, own_entry, 0, unroll=UNROLL)
+    for load in loads[:3]:
+        load.wait()
+    first_one, first_two = local_leaves, local_leaves * 3 // 2
+
+    def joined(first, transfer):
+        left = jnp.dot(
+            skel_at[0][first], transfer[:RANK], preferred_element_type=jnp.float32
+        )
+        right = jnp.dot(
+            skel_at[0][first + 1], transfer[RANK:], preferred_element_type=jnp.float32
+        )
+        return (left + right).astype(jnp.bfloat16)
+
+    for index in range(local_leaves):
+        skel_at[0][index] = jnp.dot(
+            rhs[index], basis[index], preferred_element_type=jnp.float32
+        ).astype(jnp.bfloat16)
+    for index in range(first_two - first_one):
+        skel_at[0][first_one + index] = joined(2 * index, one[index])
+    for index in range(node_count - first_two):
+        skel_at[0][first_two + index] = joined(first_one + 2 * index, two[index])
+    choose(0)
+    lax.fori_loop(0, local_leaves // 2, own_entry, 0, unroll=UNROLL)
+    by_row(more_sends)
+    lax.fori_loop(local_leaves // 2, local_leaves, own_entry, 0, unroll=UNROLL)
     for distance in range(1, rows):
         by_row(functools.partial(phase, distance=distance))
+        arrived(POINT, rows + distance - 1)
+        share_points(rows + distance - 1)
         tiles(distance)
         tiles(rows + distance - 1)
 
-    for load in loads:
-        load.wait()
+    loads[3].wait()
+    arrived(POINT, slots - 1)
+    share_points(slots - 1)
     for slot in range(rows, slots):
         arrived(SKEL, slot)
 
     def far_node(node, carry):
         total = None
         for partner in range(FAR):
-            weights = skel_at[far_tab[node * FAR + partner]]
+            weights = partners_at[far_tab[node * FAR + partner]]
             term = jnp.dot(weights, blocks[node, partner], preferred_element_type=jnp.float32)
             total = term if total is None else total + term
         far_at[node] = total
@@ -351,7 +411,6 @@
             preferred_element_type=jnp.float32,
         )
 
-    first_one, first_two = local_leaves, local_leaves * 3 // 2
     for parent in range(node_count - first_two):
         spread = spread_to(far_at[first_two + parent], two[parent])
         for child in range(2):
@@ -370,12 +429,18 @@
         out[:, index * LEAF : (index + 1) * LEAF] = total + spread_to(far_at[index], basis[index])
 
     def finish(at):
-        for kind in (POINT, SKEL, CHARGE):
-            for slot in range(slots):
-                for copy in sends(at, kind, slot):
+        for kind in (POINT, EARLY, SKEL, LATE):
+            for rank in range(rows):
+                for copy in along(at, kind, rank):
                     copy.wait_send()
 
     by_row(finish)
+    for rank in range(rows):
+        for kind in (POINT, EARLY, SKEL, LATE):
+            beside(kind, rank).wait_send()
+    for slot in range(1, slots):
+        for away in range(1, parts):
+            to_peer(slot, away).wait_send()
 
 
 UNROLL = 2
@@ -384,7 +449,9 @@
 def on_device(coords, rhs, basis, transfer_one, transfer_two, far_blocks, neighbours, far_lists):
     peer_count = lax.axis_size("leaf")
     whole_lists = peer_count == NB and peer_count % 2 == 0
-    route = gathered if whole_lists and FEAT % lax.axis_size("rhs") == 0 else exchanged
+    even_lists = far_blocks.shape[0] * FAR == (NB - 1) * basis.shape[0]
+    even_shares = FEAT % lax.axis_size("rhs") == 0
+    route = gathered if whole_lists and even_lists and even_shares else exchanged
     return route(coords, rhs, basis, transfer_one, transfer_two, far_blocks, neighbours, far_lists)
 
 
@@ -399,21 +466,10 @@
     remote_count = (NB - 1) * local_leaves
     points = coords.reshape(FEAT, local_leaves, LEAF).transpose(1, 0, 2)
     charges = rhs.reshape(R, local_leaves, LEAF).transpose(1, 0, 2)
-    skel_zero = jnp.einsum(
-        "lra,lak->lrk", charges, basis, preferred_element_type=jnp.float32
-    ).astype(jnp.bfloat16)
-    skel_one = jnp.einsum(
-        "mrj,mjk->mrk", join_pairs(skel_zero), transfer_one, preferred_element_type=jnp.float32
-    ).astype(jnp.bfloat16)
-    skel_two = jnp.einsum(
-        "mrj,mjk->mrk", join_pairs(skel_one), transfer_two, preferred_element_type=jnp.float32
-    ).astype(jnp.bfloat16)
-    skeleton = jnp.concatenate([skel_zero, skel_one, skel_two], axis=0)
-
     orders = visit_orders(rows)
     row, side = device_index // 2, device_index % 2
 
-    def slot_of(owner):
+    def slot_of(owner, side):
         origin, beside = owner // 2, (owner % 2 + side) % 2
         rank = jnp.zeros_like(owner)
         for at in range(rows):
@@ -422,18 +478,28 @@
                 rank = jnp.where(matches, place, rank)
         return beside * rows + rank
 
-    listed = lax.dynamic_slice_in_dim(neighbours, device_index * local_leaves, local_leaves, 0)
-    remote = listed[:, 1:].reshape(remote_count)
-    slot = slot_of(remote // local_leaves)
+    beside_index = device_index + 1 - 2 * side
+    lists = jnp.stack(
+        [
+            neighbours.reshape(peer_count, local_leaves, NB)[:, :, 1:].reshape(peer_count, -1)[
+                device_index
+            ],
+            far_lists.reshape(peer_count, node_count * FAR)[device_index],
+            far_lists.reshape(peer_count, node_count * FAR)[beside_index],
+        ]
+    )
+    widths = jnp.array([[local_leaves], [node_count], [node_count]], jnp.int32)
+    sides = jnp.stack([side, side, 1 - side])[:, None]
+    slot = slot_of(lists // widths, sides)
     position = jnp.arange(remote_count, dtype=jnp.int32)
-    earlier = jnp.logical_and(slot[:, None] == slot[None, :], position[None, :] < position[:, None])
-    place_tab = (slot - 1) * local_leaves + jnp.sum(earlier, axis=1, dtype=jnp.int32)
-    chosen = place_tab[None, :] == position[:, None]
-    source_tab = jnp.sum(jnp.where(chosen, (remote % local_leaves)[None, :], 0), axis=1)
-    target_tab = jnp.sum(jnp.where(chosen, (position // (NB - 1))[None, :], 0), axis=1)
-    far_listed = lax.dynamic_slice_in_dim(far_lists, device_index * node_count, node_count, 0)
-    far_listed = far_listed.reshape(node_count * FAR)
-    far_tab = (slot_of(far_listed // node_count) - 1) * node_count + far_listed % node_count
+    earlier = jnp.logical_and(
+        slot[:, :, None] == slot[:, None, :], position[None, :] < position[:, None]
+    )
+    place = (slot - 1) * local_leaves + jnp.sum(earlier, axis=2, dtype=jnp.int32)
+    chosen = place[:, None, :] == position[:, None]
+    picks = jnp.sum(jnp.where(chosen, (lists % widths)[:, None, :], 0), axis=2)
+    targets = jnp.sum(jnp.where(chosen[0], (position // (NB - 1))[None, :], 0), axis=1)
+    tables = (picks[0], targets, place[0], picks[1], picks[2], place[1])
 
     smem = pl.BlockSpec(memory_space=pltpu.SMEM)
     vmem = pl.BlockSpec(memory_space=pltpu.VMEM)
@@ -443,12 +509,14 @@
     return pl.pallas_call(
         functools.partial(whole_kernel, rows, parts),
         out_shape=jax.ShapeDtypeStruct((R, width), jnp.float32),
-        in_specs=[smem] * 4 + [vmem] * 3 + [anywhere] * 4,
+        in_specs=[smem] * 6 + [vmem] * 2 + [anywhere] * 4,
         out_specs=vmem,
         scratch_shapes=[pltpu.VMEM((local_leaves, FEAT, LEAF), bf16)] * remote_slots
         + [pltpu.VMEM((local_leaves, R, LEAF), bf16)] * remote_slots
+        + [pltpu.VMEM((node_count, R, RANK), bf16)] * rows
         + [
-            pltpu.VMEM((remote_slots * node_count, R, RANK), bf16),
+            pltpu.VMEM((rows * local_leaves, R, RANK), bf16),
+            pltpu.VMEM((remote_count, R, RANK), bf16),
             pltpu.VMEM((peer_count * local_leaves, R, LEAF), jnp.float32),
             pltpu.VMEM((node_count, R, RANK), jnp.float32),
             pltpu.VMEM(basis.shape, bf16),
@@ -456,8 +524,8 @@
             pltpu.VMEM(transfer_two.shape, bf16),
             pltpu.VMEM(far_blocks.shape, bf16),
             pltpu.SemaphoreType.DMA((4,)),
-            pltpu.SemaphoreType.DMA((3, peer_count, 3)),
-            pltpu.SemaphoreType.DMA((3, peer_count)),
+            pltpu.SemaphoreType.DMA((4, peer_count, 3)),
+            pltpu.SemaphoreType.DMA((4, peer_count)),
             pltpu.SemaphoreType.DMA((peer_count, parts - 1)),
             pltpu.SemaphoreType.DMA((peer_count, parts - 1)),
         ],
@@ -466,8 +534,7 @@
         ),
         name="whole",
     )(
-        source_tab, target_tab, place_tab, far_tab, points, charges, skeleton, basis, transfer_one,
-        transfer_two, far_blocks,
+        *tables, points, charges, basis, transfer_one, transfer_two, far_blocks,
     )
 
 

time: 116 us -> 112 us (0.966)
  Pallas kernels: 105 us -> 101 us
  local copies, waits for them, and re-layouts: 4.24 us -> 7.57 us
  matrix products: 2.77 us -> 0 us
  other arithmetic: 3.95 us -> 2.05 us
    pallas_call x1, Pallas kernels: 105 us -> 101 us  [gathered(): pl.pallas_call(functools.partial(whole_kernel, rows, parts), out_shape=ja...]
    dot_general x3 -> x0, matrix products: 2.77 us -> none  [the longest x1 2.26 us: gathered(): jnp.einsum('lra,lak->lrk', charges, basis, preferred_element_type=jnp.flo...]
    transpose x1, local copies, waits for them, and re-layouts: 1.09 us -> 2.3 us  [gathered(): charges = rhs.reshape(R, local_leaves, LEAF).transpose(1, 0, 2)]
    squeeze x0 -> x2, local copies, waits for them, and re-layouts: none -> 1.18 us  [gathered(): tables = (picks[0], targets, place[0], picks[1], picks[2], place[1])]
    unnamed x13 -> x2, local copies, waits for them, and re-layouts: 2.3 us -> 3.06 us
where the time goes in v3:
time: 112 us; the launch traced here: 111 us
  Pallas kernels  101 us (90%)
  local copies, waits for them, and re-layouts  7.57 us (7%)
  other arithmetic  2.05 us (2%)
    pallas_call x1, Pallas kernels, gathered(): pl.pallas_call(functools.partial(whole_kernel, rows, parts), out_shape=ja...  101 us
    unnamed x2, local copies, waits for them, and re-layouts  3.06 us
    transpose x1, local copies, waits for them, and re-layouts, gathered(): charges = rhs.reshape(R, local_leaves, LEAF).transpose(1, 0, 2)  2.3 us

profile of v3, /device:TPU:0, one launch (start us, length us, event | category | flops | bytes accessed | tf_op | source)
XLA Modules:
  0.0 111.0 jit_solution(8116481462589440925)
XLA Ops:
  0.0 0.1 pad_add_fusion.1
  0.1 0.8 copy.19
  0.9 0.1 slice.28
  1.0 0.1 reshape.572
  1.0 0.8 copy.16
  1.8 0.1 reshape.573
  1.9 0.9 fusion.3
  2.8 0.2 convert_reduce_fusion
  3.0 0.2 select_reduce_fusion
  3.2 0.6 slice_bitcast_fusion.2
  3.8 0.6 slice_bitcast_fusion.1
  4.4 0.7 select_reduce_fusion.1.target_tab
  5.1 2.3 %bitcast_bitcast_fusion = (bf16[8,64,512]{2,1,0:T(8,128)(2,1)}, bf16[8,64,512]{2,1,0:T(8,128)(2,1)}) fusion(bf16[8,8,8,512]{3,2,1,0:T(8,128)(2,1)} %bitcast.27, bf16[8,8,8,512]{3,2,1,0:T(8,128)(2,1)} %bitcast.28), kind=kLoop, calls=%fused_computation | loop fusion | bytes 2097152 | tf_op jit(solution)/shard_map/transpose | solution.py:468
  7.4 101.3 %whole.1 = f32[64,4096]{1,0:T(8,128)} custom-call(s32[56]{0:T(128)} %get-tuple-element.11.source_tab, s32[56]{0:T(128)} %select_reduce_fusion.1.target_tab, s32[56]{0:T(128)} %get-tuple-element.8.place_tab, s32[56]{0:T(128)} %get-tuple-element.10.pick_tab, s32[56]{0:T(128)} %get-tuple-element.9.give_tab, s32[56]{0:T(128)} %get-tuple-element.7.far_tab, ...), custom_call_target="tpu_custom_call" | custom-call | tf_op jit(solution)/shard_map/whole/pallas_call | solution.py:509
  108.7 2.3 %copy.25 = f32[64,4096]{1,0:T(8,128)} copy(f32[64,4096]{1,0:T(8,128)} %whole.1) | data formatting | bytes 2097152
  (5 shorter events, 0.1 us)

commit v4 on v3

--- a/solution.py
+++ b/solution.py
@@ -175,7 +175,7 @@
 
 
 def whole_kernel(
-    rows, parts, source_tab, target_tab, place_tab, pick_tab, give_tab, far_tab, coords, rhs, basis_hbm,
+    rows, parts, source_tab, target_tab, place_tab, pick_tab, give_tab, far_tab, block_tab, coords, rhs, basis_hbm,
     one_hbm, two_hbm, blocks_hbm, out, *scratch
 ):
     slots = 2 * rows
@@ -183,11 +183,11 @@
     charges_at = (None,) + scratch[slots - 1 : 2 * slots - 2]
     skel_at = scratch[2 * slots - 2 : 2 * slots - 2 + rows]
     (
-        given, partners_at, terms, far_at, basis, one, two, blocks, local_sem, send_sem,
+        given, partners_at, far_out, terms, far_at, basis, one, two, blocks, local_sem, send_sem,
         recv_sem, peer_send_sem, peer_recv_sem,
     ) = scratch[2 * slots - 2 + rows :]
     orders = visit_orders(rows)
-    local_leaves, node_count = basis.shape[0], blocks.shape[0]
+    local_leaves, node_count = basis.shape[0], blocks.shape[0] // FAR
     share = coords.shape[1] // parts
     leaf = lax.axis_index("leaf")
     row, side = leaf // 2, leaf % 2
@@ -309,14 +309,20 @@
             start_along(kind, [0], at)
             beside(kind, 0).start()
 
-    def phase(at, distance):
-        ranks = [rank for rank in range(rows) if abs(orders[at][rank] - at) == distance]
+    def ranks_at(at, distance):
+        return [rank for rank in range(rows) if abs(orders[at][rank] - at) == distance]
+
+    def first_phase(at, distance):
+        ranks = ranks_at(at, distance)
         for kind in (POINT, EARLY):
             start_along(kind, ranks, at)
             for rank in ranks:
                 beside(kind, rank).start()
                 if kind == POINT:
                     share_points(rank)
+
+    def second_phase(at, distance):
+        ranks = ranks_at(at, distance)
         start_along(SKEL, ranks, at)
         for rank in ranks:
             choose(rank)
@@ -343,6 +349,18 @@
             target = coords[target_tab[where]]
             charge = charges_at[slot][source_tab[where]]
             terms[where] = tile(source, target, half_square(target), charge)
+            return carry
+
+        lax.fori_loop(0, local_leaves, entry, 0, unroll=UNROLL)
+
+    def far_terms(slot):
+        first = (slot - 1) * local_leaves
+
+        def entry(index, carry):
+            where = first + index
+            far_out[where] = jnp.dot(
+                partners_at[where], blocks[block_tab[where]], preferred_element_type=jnp.float32
+            )
             return carry
 
         lax.fori_loop(0, local_leaves, entry, 0, unroll=UNROLL)
@@ -382,28 +400,30 @@
     by_row(more_sends)
     lax.fori_loop(local_leaves // 2, local_leaves, own_entry, 0, unroll=UNROLL)
     for distance in range(1, rows):
-        by_row(functools.partial(phase, distance=distance))
+        by_row(functools.partial(first_phase, distance=distance))
         arrived(POINT, rows + distance - 1)
         share_points(rows + distance - 1)
+        if distance > 1:
+            tiles(rows + distance - 1)
+        by_row(functools.partial(second_phase, distance=distance))
+        if distance == 1:
+            loads[3].wait()
         tiles(distance)
-        tiles(rows + distance - 1)
-
-    loads[3].wait()
+        far_terms(distance)
+        if distance == 1:
+            tiles(rows)
+        arrived(SKEL, rows + distance - 1)
+        far_terms(rows + distance - 1)
     arrived(POINT, slots - 1)
     share_points(slots - 1)
-    for slot in range(rows, slots):
-        arrived(SKEL, slot)
-
-    def far_node(node, carry):
-        total = None
-        for partner in range(FAR):
-            weights = partners_at[far_tab[node * FAR + partner]]
-            term = jnp.dot(weights, blocks[node, partner], preferred_element_type=jnp.float32)
-            total = term if total is None else total + term
+    arrived(SKEL, slots - 1)
+    far_terms(slots - 1)
+
+    for node in range(node_count):
+        total = far_out[far_tab[node * FAR]]
+        for partner in range(1, FAR):
+            total = total + far_out[far_tab[node * FAR + partner]]
         far_at[node] = total
-        return carry
-
-    lax.fori_loop(0, node_count, far_node, 0, unroll=2)
 
     def spread_to(parent, transfer):
         return lax.dot_general(
@@ -443,7 +463,7 @@
             to_peer(slot, away).wait_send()
 
 
-UNROLL = 2
+UNROLL = 4
 
 
 def on_device(coords, rhs, basis, transfer_one, transfer_two, far_blocks, neighbours, far_lists):
@@ -498,8 +518,10 @@
     place = (slot - 1) * local_leaves + jnp.sum(earlier, axis=2, dtype=jnp.int32)
     chosen = place[:, None, :] == position[:, None]
     picks = jnp.sum(jnp.where(chosen, (lists % widths)[:, None, :], 0), axis=2)
-    targets = jnp.sum(jnp.where(chosen[0], (position // (NB - 1))[None, :], 0), axis=1)
-    tables = (picks[0], targets, place[0], picks[1], picks[2], place[1])
+    entries = jnp.sum(jnp.where(chosen[:2], position, 0), axis=2)
+    tables = (
+        picks[0], entries[0] // (NB - 1), place[0], picks[1], picks[2], place[1], entries[1]
+    )
 
     smem = pl.BlockSpec(memory_space=pltpu.SMEM)
     vmem = pl.BlockSpec(memory_space=pltpu.VMEM)
@@ -509,7 +531,7 @@
     return pl.pallas_call(
         functools.partial(whole_kernel, rows, parts),
         out_shape=jax.ShapeDtypeStruct((R, width), jnp.float32),
-        in_specs=[smem] * 6 + [vmem] * 2 + [anywhere] * 4,
+        in_specs=[smem] * 7 + [vmem] * 2 + [anywhere] * 4,
         out_specs=vmem,
         scratch_shapes=[pltpu.VMEM((local_leaves, FEAT, LEAF), bf16)] * remote_slots
         + [pltpu.VMEM((local_leaves, R, LEAF), bf16)] * remote_slots
@@ -517,12 +539,13 @@
         + [
             pltpu.VMEM((rows * local_leaves, R, RANK), bf16),
             pltpu.VMEM((remote_count, R, RANK), bf16),
+            pltpu.VMEM((remote_count, R, RANK), jnp.float32),
             pltpu.VMEM((peer_count * local_leaves, R, LEAF), jnp.float32),
             pltpu.VMEM((node_count, R, RANK), jnp.float32),
             pltpu.VMEM(basis.shape, bf16),
             pltpu.VMEM(transfer_one.shape, bf16),
             pltpu.VMEM(transfer_two.shape, bf16),
-            pltpu.VMEM(far_blocks.shape, bf16),
+            pltpu.VMEM((node_count * FAR, RANK, RANK), bf16),
             pltpu.SemaphoreType.DMA((4,)),
             pltpu.SemaphoreType.DMA((4, peer_count, 3)),
             pltpu.SemaphoreType.DMA((4, peer_count)),
@@ -534,7 +557,8 @@
         ),
         name="whole",
     )(
-        *tables, points, charges, basis, transfer_one, transfer_two, far_blocks,
+        *tables, points, charges, basis, transfer_one, transfer_two,
+        far_blocks.reshape(node_count * FAR, RANK, RANK),
     )
 
 

time: 112 us -> 109 us (0.973)
  Pallas kernels: 101 us -> 98.2 us
    pallas_call x1, Pallas kernels: 101 us -> 98.2 us  [gathered(): pl.pallas_call(functools.partial(whole_kernel, rows, parts), out_shape=ja...]
where the time goes in v4:
time: 109 us; the launch traced here: 108 us
  Pallas kernels  98.2 us (90%)
  local copies, waits for them, and re-layouts  8.11 us (7%)
  other arithmetic  2.05 us (2%)
    pallas_call x1, Pallas kernels, gathered(): pl.pallas_call(functools.partial(whole_kernel, rows, parts), out_shape=ja...  98.2 us
    unnamed x2, local copies, waits for them, and re-layouts  3.06 us
    transpose x1, local copies, waits for them, and re-layouts, gathered(): charges = rhs.reshape(R, local_leaves, LEAF).transpose(1, 0, 2)  2.3 us

profile of v4, /device:TPU:0, one launch (start us, length us, event | category | flops | bytes accessed | tf_op | source)
XLA Modules:
  0.0 108.4 jit_solution(334925810110626077)
XLA Ops:
  0.0 0.1 pad_add_fusion.1
  0.1 0.8 copy.19
  0.9 0.1 slice.36
  0.9 0.1 reshape.572
  1.0 0.8 copy.16
  1.8 0.1 reshape.573
  1.9 0.9 fusion.3
  2.8 0.2 convert_reduce_fusion
  3.0 0.2 select_reduce_fusion
  3.2 0.6 slice_bitcast_fusion.2
  3.8 0.6 slice_bitcast_fusion.1
  4.4 0.1 select_reduce_fusion.1
  4.5 0.5 slice_bitcast_fusion.block_tab
  5.0 0.6 bitcast_select_fusion.target_tab
  5.6 2.3 %bitcast_bitcast_fusion = (bf16[8,64,512]{2,1,0:T(8,128)(2,1)}, bf16[8,64,512]{2,1,0:T(8,128)(2,1)}) fusion(bf16[8,8,8,512]{3,2,1,0:T(8,128)(2,1)} %bitcast.31, bf16[8,8,8,512]{3,2,1,0:T(8,128)(2,1)} %bitcast.32), kind=kLoop, calls=%fused_computation | loop fusion | bytes 2097152 | tf_op jit(solution)/shard_map/transpose | solution.py:488
  7.9 98.2 %whole.1 = f32[64,4096]{1,0:T(8,128)} custom-call(s32[56]{0:T(128)} %get-tuple-element.11.source_tab, s32[56]{0:T(128)} %bitcast_select_fusion.target_tab, s32[56]{0:T(128)} %get-tuple-element.8.place_tab, s32[56]{0:T(128)} %get-tuple-element.10.pick_tab, s32[56]{0:T(128)} %get-tuple-element.9.give_tab, s32[56]{0:T(128)} %get-tuple-element.7.far_tab, ...), custom_call_target="tpu_custom_call" | custom-call | tf_op jit(solution)/shard_map/whole/pallas_call | solution.py:531
  106.2 2.3 %copy.25 = f32[64,4096]{1,0:T(8,128)} copy(f32[64,4096]{1,0:T(8,128)} %whole.1) | data formatting | bytes 2097152
  (4 shorter events, 0.0 us)

commit v5 on v4

--- a/solution.py
+++ b/solution.py
@@ -175,7 +175,7 @@
 
 
 def whole_kernel(
-    rows, parts, source_tab, target_tab, place_tab, pick_tab, give_tab, far_tab, block_tab, coords, rhs, basis_hbm,
+    rows, parts, picks, places, entries, coords_hbm, rhs_hbm, basis_hbm,
     one_hbm, two_hbm, blocks_hbm, out, *scratch
 ):
     slots = 2 * rows
@@ -183,7 +183,7 @@
     charges_at = (None,) + scratch[slots - 1 : 2 * slots - 2]
     skel_at = scratch[2 * slots - 2 : 2 * slots - 2 + rows]
     (
-        given, partners_at, far_out, terms, far_at, basis, one, two, blocks, local_sem, send_sem,
+        coords, rhs, given, partners_at, far_out, terms, far_at, basis, one, two, blocks, local_sem, leaf_sem, send_sem,
         recv_sem, peer_send_sem, peer_recv_sem,
     ) = scratch[2 * slots - 2 + rows :]
     orders = visit_orders(rows)
@@ -200,7 +200,14 @@
             ((basis_hbm, basis), (one_hbm, one), (two_hbm, two), (blocks_hbm, blocks))
         )
     ]
-    for load in loads:
+    leaf_loads = [
+        pltpu.make_async_copy(
+            source.at[:, pl.ds(index * LEAF, LEAF)], target.at[index], leaf_sem.at[which, index]
+        )
+        for which, (source, target) in enumerate(((coords_hbm, coords), (rhs_hbm, rhs)))
+        for index in range(local_leaves)
+    ]
+    for load in leaf_loads + loads:
         load.start()
 
     barrier = pltpu.get_barrier_semaphore()
@@ -284,10 +291,10 @@
     def choose(rank):
         def entry(index, carry):
             place = rank * local_leaves + index
-            given[place] = skel_at[rank][give_tab[rows * local_leaves - local_leaves + place]]
+            given[place] = skel_at[rank][picks[2, rows * local_leaves - local_leaves + place]]
             if rank > 0:
                 taken = place - local_leaves
-                partners_at[taken] = skel_at[rank][pick_tab[taken]]
+                partners_at[taken] = skel_at[rank][picks[1, taken]]
             return carry
 
         lax.fori_loop(0, local_leaves, entry, 0)
@@ -345,9 +352,9 @@
 
         def entry(index, carry):
             where = first + index
-            source = points_at[slot][source_tab[where]]
-            target = coords[target_tab[where]]
-            charge = charges_at[slot][source_tab[where]]
+            source = points_at[slot][picks[0, where]]
+            target = coords[entries[0, where]]
+            charge = charges_at[slot][picks[0, where]]
             terms[where] = tile(source, target, half_square(target), charge)
             return carry
 
@@ -359,12 +366,14 @@
         def entry(index, carry):
             where = first + index
             far_out[where] = jnp.dot(
-                partners_at[where], blocks[block_tab[where]], preferred_element_type=jnp.float32
+                partners_at[where], blocks[entries[1, where]], preferred_element_type=jnp.float32
             )
             return carry
 
         lax.fori_loop(0, local_leaves, entry, 0, unroll=UNROLL)
 
+    for load in leaf_loads:
+        load.wait()
     by_row(open_sends)
 
     own_first = (slots - 1) * local_leaves
@@ -420,9 +429,9 @@
     far_terms(slots - 1)
 
     for node in range(node_count):
-        total = far_out[far_tab[node * FAR]]
+        total = far_out[places[1, node * FAR]]
         for partner in range(1, FAR):
-            total = total + far_out[far_tab[node * FAR + partner]]
+            total = total + far_out[places[1, node * FAR + partner]]
         far_at[node] = total
 
     def spread_to(parent, transfer):
@@ -445,7 +454,7 @@
     for index in range(local_leaves):
         total = terms[own_first + index]
         for listed in range(NB - 1):
-            total = total + terms[place_tab[index * (NB - 1) + listed]]
+            total = total + terms[places[0, index * (NB - 1) + listed]]
         out[:, index * LEAF : (index + 1) * LEAF] = total + spread_to(far_at[index], basis[index])
 
     def finish(at):
@@ -484,8 +493,6 @@
     node_count = far_blocks.shape[0]
     width = rhs.shape[1]
     remote_count = (NB - 1) * local_leaves
-    points = coords.reshape(FEAT, local_leaves, LEAF).transpose(1, 0, 2)
-    charges = rhs.reshape(R, local_leaves, LEAF).transpose(1, 0, 2)
     orders = visit_orders(rows)
     row, side = device_index // 2, device_index % 2
 
@@ -519,9 +526,8 @@
     chosen = place[:, None, :] == position[:, None]
     picks = jnp.sum(jnp.where(chosen, (lists % widths)[:, None, :], 0), axis=2)
     entries = jnp.sum(jnp.where(chosen[:2], position, 0), axis=2)
-    tables = (
-        picks[0], entries[0] // (NB - 1), place[0], picks[1], picks[2], place[1], entries[1]
-    )
+    divisors = jnp.array([[NB - 1], [1]], jnp.int32)
+    tables = (picks, place, entries // divisors)
 
     smem = pl.BlockSpec(memory_space=pltpu.SMEM)
     vmem = pl.BlockSpec(memory_space=pltpu.VMEM)
@@ -531,12 +537,14 @@
     return pl.pallas_call(
         functools.partial(whole_kernel, rows, parts),
         out_shape=jax.ShapeDtypeStruct((R, width), jnp.float32),
-        in_specs=[smem] * 7 + [vmem] * 2 + [anywhere] * 4,
+        in_specs=[smem] * 3 + [anywhere] * 6,
         out_specs=vmem,
         scratch_shapes=[pltpu.VMEM((local_leaves, FEAT, LEAF), bf16)] * remote_slots
         + [pltpu.VMEM((local_leaves, R, LEAF), bf16)] * remote_slots
         + [pltpu.VMEM((node_count, R, RANK), bf16)] * rows
         + [
+            pltpu.VMEM((local_leaves, FEAT, LEAF), bf16),
+            pltpu.VMEM((local_leaves, R, LEAF), bf16),
             pltpu.VMEM((rows * local_leaves, R, RANK), bf16),
             pltpu.VMEM((remote_count, R, RANK), bf16),
             pltpu.VMEM((remote_count, R, RANK), jnp.float32),
@@ -547,6 +555,7 @@
             pltpu.VMEM(transfer_two.shape, bf16),
             pltpu.VMEM((node_count * FAR, RANK, RANK), bf16),
             pltpu.SemaphoreType.DMA((4,)),
+            pltpu.SemaphoreType.DMA((2, local_leaves)),
             pltpu.SemaphoreType.DMA((4, peer_count, 3)),
             pltpu.SemaphoreType.DMA((4, peer_count)),
             pltpu.SemaphoreType.DMA((peer_count, parts - 1)),
@@ -557,7 +566,7 @@
         ),
         name="whole",
     )(
-        *tables, points, charges, basis, transfer_one, transfer_two,
+        *tables, coords, rhs, basis, transfer_one, transfer_two,
         far_blocks.reshape(node_count * FAR, RANK, RANK),
     )
 

time: 109 us -> 106 us (0.972)
  local copies, waits for them, and re-layouts: 8.11 us -> 4.08 us
  other arithmetic: 2.05 us -> 3.48 us
    transpose x1 -> x0, local copies, waits for them, and re-layouts: 2.3 us -> none  [gathered(): charges = rhs.reshape(R, local_leaves, LEAF).transpose(1, 0, 2)]
    squeeze x3 -> x0, local copies, waits for them, and re-layouts: 1.72 us -> none  [the longest x1 0.59 us: gathered(): place[1]]
    unnamed x2 -> x4, local copies, waits for them, and re-layouts: 3.06 us -> 3.06 us
where the time goes in v5:
time: 106 us
  Pallas kernels  98.2 us (93%)
  local copies, waits for them, and re-layouts  4.08 us (4%)
  other arithmetic  3.48 us (3%)
    pallas_call x1, Pallas kernels, gathered(): pl.pallas_call(functools.partial(whole_kernel, rows, parts), out_shape=ja...  98.2 us
    unnamed x4, local copies, waits for them, and re-layouts  3.06 us

profile of v5, /device:TPU:0, one launch (start us, length us, event | category | flops | bytes accessed | tf_op | source)
XLA Modules:
  0.0 105.8 jit_solution(9743939469513608274)
XLA Ops:
  0.0 0.1 pad_add_fusion.1
  0.1 0.8 copy.17
  0.9 0.1 slice.8
  0.9 0.1 reshape.556
  1.0 0.8 copy.16
  1.8 0.1 reshape.557
  1.9 0.9 fusion.3
  2.8 0.2 convert_reduce_fusion
  3.0 0.0 copy-start
  3.0 0.7 select_reduce_fusion.picks
  3.8 0.1 select_reduce_fusion.1
  3.9 1.4 %and_select_fusion.entries = s32[2,56]{1,0:T(2,128)} fusion(s32[2,56]{1,0:T(2,128)S(1)} %select_reduce_fusion.1, s32[2]{0:T(128)} %constant.109), kind=kLoop, calls=%fused_computation.25 | loop fusion | flops 896 | bytes 904 | tf_op jit(solution)/shard_map/jit(floor_divide)/jit(_where)/select_n | solution.py:530
  5.3 0.0 copy-done
  5.3 98.2 %whole.1 = f32[64,4096]{1,0:T(8,128)} custom-call(s32[3,56]{1,0:T(4,128)} %select_reduce_fusion.picks, s32[3,56]{1,0:T(4,128)} %copy-done, s32[2,56]{1,0:T(2,128)} %and_select_fusion.entries, bf16[64,4096]{1,0:T(8,128)(2,1)} %coords_hbm.1, bf16[64,4096]{1,0:T(8,128)(2,1)} %rhs_hbm.1, bf16[8,512,256]{2,1,0:T(8,128)(2,1)} %basis_hbm.1, ...), custom_call_target="tpu_custom_call" | custom-call | tf_op jit(solution)/shard_map/whole/pallas_call | solution.py:537
  103.5 2.3 %copy.19 = f32[64,4096]{1,0:T(8,128)} copy(f32[64,4096]{1,0:T(8,128)} %whole.1) | data formatting | bytes 2097152
  (4 shorter events, 0.0 us)
Async XLA Ops:
  3.0 2.3 %copy-start = (s32[3,56]{1,0:T(4,128)}, s32[3,56]{1,0:T(4,128)S(1)}, u32[]{:S(2)}) copy-start(s32[3,56]{1,0:T(4,128)S(1)} %multiply_add_fusion.places) | copy-start | bytes 2020
